TPU v7x, 32 devices: a whole 2x2x4 slice. The times are simulated.
32 devices in a mesh: section: 2 (over core), dp: 4 (over z), mp: 4 (over y, x).
Axes of the slice: x: 2, y: 2, z: 4, core: 2. Of those that a mesh axis runs over, the one named last changes fastest.
Arguments:
- states: bfloat16 [2, 512, 4096], P('section', 'dp'), may hold values from -6 to 6
- gains: float32 [2, 4096], P('section'), may hold values from 0.25 to 1.75
- proj_a: bfloat16 [2, 4096, 4096], P('section', None, 'mp'), may hold values from -0.03125 to 0.03125
- proj_b: bfloat16 [2, 4096, 4096], P('section', None, 'mp'), may hold values from -0.09375 to 0.09375
- cotangent: bfloat16 [512, 4096], P('dp'), may hold values from -12 to 12
- src_len: int32 [4, 16], replicated, may hold values from 1 to 16, 128 in all within a row
- tgt_len: int32 [4, 16], replicated, may hold values from 1 to 16, 128 in all within a row
- dest: int32 [4, 16], replicated, may hold values from 0 to 63, as said below
Outputs:
- grad_states: bfloat16 [2, 512, 4096], P('section', 'dp')
- grad_a: float32 [2, 4096, 4096], P('section', 'dp', 'mp')
- grad_b: float32 [2, 4096, 4096], P('section', 'dp', 'mp')
Inputs may be any that keep to these rules, and one draw needn't show every extreme that they name: `src_len`: each row sums to 128. `tgt_len`: each row sums to 128. `dest`: every value from 0 to 63 appears once; each row holds exactly 4 values in each range d * 16 to (d + 1) * 16 - 1.
All inputs are finite; a program needn't handle non-finite values.
Results may differ from a plain program's by a relative error of at most 0.014.
Values may be sent and summed in bfloat16 or wider, within the bound.
A program may use at most 128 MiB of HBM per device.

v0:
```python
import jax
import jax.numpy as jnp
from jax import lax
from jax.sharding import PartitionSpec as P

HEAD_DIM = 64
SEQ_DEV = 16
MAXLEN = 16


EPS = 1e-06


def swapped(shard, axis, apart):
    return lax.ppermute(shard, axis, [(i, i ^ 1 << apart) for i in range(lax.axis_size(axis))])


def rms_forward(states_row, gain):
    xf = states_row.astype(jnp.float32)
    scale = lax.rsqrt(jnp.mean(xf * xf, axis=-1, keepdims=True) + EPS)
    return (xf, scale, (xf * scale * gain).astype(jnp.bfloat16))


def rms_backward(xf, scale, gain, dnorm):
    upper = gain * dnorm
    inner = jnp.mean(xf * upper, axis=-1, keepdims=True)
    return (scale * upper - xf * scale * scale * scale * inner).astype(jnp.bfloat16)


def route(slots):
    return lax.all_to_all(slots, "dp", split_axis=0, concat_axis=0, tiled=True)


def cross_groups(slots):
    return swapped(slots, "section", 0)


def pack(rows, starts, lengths, picked):
    steps = jnp.arange(MAXLEN, dtype=jnp.int32)
    index = starts[picked][:, None] + steps[None, :]
    valid = steps[None, :] < lengths[picked][:, None]
    taken = rows[jnp.minimum(index, rows.shape[0] - 1)]
    return jnp.where(valid[:, :, None], taken, jnp.zeros((), rows.dtype))


def unpack(padded, starts, lengths, picked, tokens):
    ends = starts + lengths
    place = jnp.arange(tokens, dtype=jnp.int32)
    which = jnp.sum((place[:, None] >= ends[None, :]).astype(jnp.int32), axis=-1)
    position = jnp.argsort(picked)
    flat = position[which] * MAXLEN + place - starts[which]
    return padded.reshape(-1, padded.shape[-1])[flat]


def spare(own, remote, key_len):
    return (jnp.zeros_like(own), jnp.zeros_like(own))


def attend(own, remote, key_len):
    seqs, length, width = own.shape
    cols = width // 2
    heads = cols // HEAD_DIM
    query = own[..., :cols].reshape(seqs, length, heads, HEAD_DIM)
    dout = own[..., cols:].reshape(seqs, length, heads, HEAD_DIM)
    keys = remote[..., :cols].reshape(seqs, length, heads, HEAD_DIM)
    values = remote[..., cols:].reshape(seqs, length, heads, HEAD_DIM)
    scores = jnp.einsum("sqhd,skhd->shqk", query, keys, preferred_element_type=jnp.float32)
    live = jnp.arange(length, dtype=jnp.int32)[None, None, None, :] < key_len[:, None, None, None]
    expo = jnp.where(live, jnp.exp(scores), jnp.float32(0.0))
    weight = expo / jnp.sum(expo, axis=-1, keepdims=True)
    weight_b = weight.astype(jnp.bfloat16)
    attended = jnp.einsum(
        "shqk,skhd->sqhd", weight_b, values, preferred_element_type=jnp.float32
    ).astype(jnp.bfloat16)
    dweight = jnp.einsum("sqhd,skhd->shqk", dout, values, preferred_element_type=jnp.float32)
    total = jnp.sum(weight * dweight, axis=-1, keepdims=True)
    dscore = (weight * (dweight - total)).astype(jnp.bfloat16)
    dquery = jnp.einsum("shqk,skhd->sqhd", dscore, keys, preferred_element_type=jnp.float32).astype(
        jnp.bfloat16
    )
    dkeys = jnp.einsum("shqk,sqhd->skhd", dscore, query, preferred_element_type=jnp.float32).astype(
        jnp.bfloat16
    )
    dvalues = jnp.einsum(
        "shqk,sqhd->skhd", weight_b, dout, preferred_element_type=jnp.float32
    ).astype(jnp.bfloat16)
    front = jnp.concatenate(
        [dquery.reshape(seqs, length, cols), attended.reshape(seqs, length, cols)], axis=-1
    )
    back = jnp.concatenate(
        [dkeys.reshape(seqs, length, cols), dvalues.reshape(seqs, length, cols)], axis=-1
    )
    return (front, back)


def left_product(left, right):
    return lax.dot_general(
        left, right, (((0,), (0,)), ((), ())), preferred_element_type=jnp.float32
    )


def right_product(rows, weight):
    return lax.dot_general(
        rows, weight, (((1,), (1,)), ((), ())), preferred_element_type=jnp.float32
    )


def per_device(states, gains, proj_a, proj_b, cotangent, src_len, tgt_len, dest):
    encoder = lax.axis_index("section") == 0
    member = lax.axis_index("dp")
    members = lax.axis_size("dp")
    group = SEQ_DEV // members
    gain = gains[0]
    weight_a = proj_a[0]
    weight_b = proj_b[0]
    cols = weight_a.shape[1]
    tokens = states.shape[1]
    xf, scale, normed = rms_forward(states[0], gain)
    second_left = jnp.where(encoder, normed, cotangent)
    first = jnp.dot(normed, weight_a, preferred_element_type=jnp.float32).astype(jnp.bfloat16)
    second = jnp.dot(second_left, weight_b, preferred_element_type=jnp.float32).astype(jnp.bfloat16)
    paired = jnp.concatenate([first, second], axis=1)
    order = jnp.argsort(dest, axis=1)
    sorted_dest = jnp.take_along_axis(dest, order, axis=1)
    sorted_len = jnp.take_along_axis(src_len, order, axis=1)
    begin = member * group
    anchor = jnp.int32(0)
    incoming = (
        lax.dynamic_slice(sorted_dest, (anchor, begin), (members, group)).reshape(-1)
        - member * SEQ_DEV
    )
    key_len = lax.dynamic_slice(sorted_len, (anchor, begin), (members, group)).reshape(-1)
    picked = jnp.where(encoder, order[member], incoming)
    lengths = jnp.where(encoder, src_len[member], tgt_len[member])
    starts = jnp.cumsum(lengths) - lengths
    slots = pack(paired, starts, lengths, picked)
    remote = cross_groups(route(slots))
    front, back = lax.cond(encoder, spare, attend, slots, remote, key_len)
    returned = route(cross_groups(back))
    padded = jnp.where(encoder, returned, front)
    rows = unpack(padded, starts, lengths, picked, tokens)
    grad_first = rows[:, :cols]
    grad_second = rows[:, cols:]
    used_second = jnp.where(encoder, grad_second, jnp.zeros((), jnp.bfloat16))
    partial_norm = right_product(grad_first, weight_a) + right_product(used_second, weight_b)
    dnorm = lax.psum(partial_norm, "mp")
    grad_states = rms_backward(xf, scale, gain, dnorm)
    mine_a, mine_b = (
        lax.all_to_all(normed, "dp", split_axis=1, concat_axis=0, tiled=True),
        lax.all_to_all(second_left, "dp", split_axis=1, concat_axis=0, tiled=True),
    )
    grad_a = left_product(mine_a, lax.all_gather(grad_first, "dp", axis=0, tiled=True))
    grad_b = left_product(mine_b, lax.all_gather(grad_second, "dp", axis=0, tiled=True))
    return (grad_states[None], grad_a[None], grad_b[None])


def solution(mesh):
    return jax.shard_map(
        per_device,
        mesh=mesh,
        in_specs=(
            P("section", "dp", None),
            P("section", None),
            P("section", None, "mp"),
            P("section", None, "mp"),
            P("dp", None),
            P(),
            P(),
            P(),
        ),
        out_specs=(P("section", "dp", None), P("section", "dp", "mp"), P("section", "dp", "mp")),
        check_vma=False,
    )
```

profile of v0, /device:TPU:0, one launch (start us, length us, event | category | flops | bytes accessed | tf_op | source)
XLA Modules:
  0.0 245.2 jit_solution(6942427891484860981)
XLA Ops:
  9.5 1.5 fusion.31
  11.2 5.2 %fusion.44 = bf16[128,1024]{1,0:T(8,128)(2,1)S(1)} fusion(bf16[1,4096,1024]{2,1,0:T(8,128)(2,1)} %param.14, bf16[1,128,4096]{2,1,0:T(8,128)(2,1)} %param.12, f32[4096]{0:T(1024)} %bitcast.371, f32[128]{0:T(128)S(1)} %add_rsqrt_fusion), kind=kOutput, calls=%fused_computation.65 | convolution fusion | flops 1075970048 | bytes 9716224 | tf_op jit(solution)/shard_map/dot_general | solution.py:120
  18.2 0.9 gather_fusion.5
  21.2 4.7 %fusion.47 = bf16[128,1024]{1,0:T(8,128)(2,1)S(1)} fusion(bf16[128,4096]{1,0:T(8,128)(2,1)S(1)} %fusion.53, bf16[1,4096,1024]{2,1,0:T(8,128)(2,1)} %param.15), kind=kOutput, calls=%fused_computation.66 | convolution fusion | flops 1073872896 | bytes 9699328 | tf_op jit(solution)/shard_map/dot_general | solution.py:121
  25.9 2.3 gather_fusion.2
  28.3 1.4 broadcast_select_fusion
  29.6 31.9 %all_to_all.45 = bf16[16,16,2048]{2,1,0:T(8,128)(2,1)S(1)} all-to-all(bf16[16,16,2048]{2,1,0:T(8,128)(2,1)S(1)} %broadcast_select_fusion), channel_id=1, replica_groups=mesh['section'=2,'dp'=4,'mp'=4] {'dp'}, dimensions={0} | all-to-all | bytes 2097152 | tf_op jit(solution)/shard_map/all_to_all | solution.py:31
  62.4 1.9 collective-permute-done
  64.3 1.2 conditional.1
  64.3 1.1 broadcast.200
  65.5 32.6 %collective-permute-start.1 = (bf16[16,16,2048]{2,1,0:T(8,128)(2,1)S(1)}, bf16[16,16,2048]{2,1,0:T(8,128)(2,1)}, u32[]{:S(2)}, u32[]{:S(2)}) collective-permute-start(bf16[16,16,2048]{2,1,0:T(8,128)(2,1)S(1)} %get-tuple-element.31), channel_id=1, source_target_pairs={{0,16},{16,0},{1,17},{17,1},{2,18},{18,2},{3,19},{19,3},{4,20},{20... | collective-permute-start | bytes 3145736 | tf_op jit(solution)/shard_map/ppermute | solution.py:15
  98.1 2.4 collective-permute-done.1
  100.5 3.5 %all-to-all-start.1 = ((bf16[16,16,2048]{2,1,0:T(8,128)(2,1)}), bf16[16,16,2048]{2,1,0:T(8,128)(2,1)S(1)}, u32[]{:S(2)}, u32[]{:S(2)}) async-start(bf16[16,16,2048]{2,1,0:T(8,128)(2,1)} %collective-permute-done.1), calls=%async_computation.1 | async-start | bytes 2097152 | tf_op jit(solution)/shard_map/all_to_all | solution.py:31
  104.2 1.2 sort.35
  106.9 20.0 %fusion.66 = s32[128]{0:T(128)S(1)} fusion(s32[128]{0:T(128)S(1)} %convert_reduce_fusion, s32[]{:T(128)} %bitcast.53, s32[]{:T(128)} %bitcast.35, s32[]{:T(128)} %bitcast.54, s32[]{:T(128)} %bitcast.36, s32[]{:T(128)} %bitcast.55, s32[]{:T(128)} %bitcast.37, s32[]{:T(128)} %bitcast.56, s32[]{:T(128)} %bitcast.38, s32[]{:T(128)} %bitcast.57, s32[]{:T(128)} %bitcast.39, ...), kind=kLoop, calls=%fused_computation.138 | loop fusion | flops 6912 | bytes 1152 | tf_op jit(solution)/shard_map/select_n | solution.py:52
  126.9 3.6 %all-to-all-done.1 = bf16[16,16,2048]{2,1,0:T(8,128)(2,1)S(1)} async-done(((bf16[16,16,2048]{2,1,0:T(8,128)(2,1)}), bf16[16,16,2048]{2,1,0:T(8,128)(2,1)S(1)}, u32[]{:S(2)}, u32[]{:S(2)}) %all-to-all-start.1) | async-done | bytes 1048608 | tf_op jit(solution)/shard_map/all_to_all | solution.py:31
  130.7 0.9 gather_fusion.3
  131.6 0.9 fusion.73
  132.6 1.7 reshape.309
  135.6 2.2 fusion.34
  137.7 3.7 %all-to-all-start.2 = ((bf16[128,4,1024]{2,0,1:T(8,128)(2,1)}), bf16[128,4,1024]{2,0,1:T(8,128)(2,1)S(1)}, u32[]{:S(2)}, u32[]{:S(2)}) async-start(bf16[128,4,1024]{2,0,1:T(8,128)(2,1)} %fusion.34), calls=%async_computation.2 | async-start | bytes 2097152 | tf_op jit(solution)/shard_map/all_to_all | solution.py:149
  141.5 6.3 %fusion.20 = f32[128,4096]{1,0:T(8,128)S(1)} fusion(bf16[1,4096,1024]{2,1,0:T(8,128)(2,1)} %param.15, pred[]{:T(512)S(6)} %eq.3, bf16[128,2048]{1,0:T(8,128)(2,1)S(1)} %copy-done.7), kind=kOutput, calls=%fused_computation.36 | convolution fusion | flops 1073872896 | bytes 10747905 | tf_op jit(solution)/shard_map/dot_general | solution.py:103
  147.8 7.6 %fusion.28 = f32[128,4096]{1,0:T(8,128)} fusion(f32[128,4096]{1,0:T(8,128)S(1)} %fusion.20, bf16[1,4096,1024]{2,1,0:T(8,128)(2,1)} %param.14, bf16[128,2048]{1,0:T(8,128)(2,1)S(1)} %copy-done.7), kind=kOutput, calls=%fused_computation.44 | convolution fusion | flops 1074266112 | bytes 12845056 | tf_op jit(solution)/shard_map/dot_general | solution.py:103
  155.4 1.2 copy-done.4
  156.6 1.1 copy.126
  157.6 25.1 %all-to-all-done.2 = bf16[128,4,1024]{2,0,1:T(8,128)(2,1)S(1)} async-done(((bf16[128,4,1024]{2,0,1:T(8,128)(2,1)}), bf16[128,4,1024]{2,0,1:T(8,128)(2,1)S(1)}, u32[]{:S(2)}, u32[]{:S(2)}) %all-to-all-start.2) | async-done | bytes 1048608 | tf_op jit(solution)/shard_map/all_to_all | solution.py:149
  182.7 3.5 %all-to-all-start.3 = ((bf16[128,4,1024]{2,0,1:T(8,128)(2,1)}), bf16[128,4,1024]{2,0,1:T(8,128)(2,1)S(1)}, u32[]{:S(2)}, u32[]{:S(2)}) async-start(bf16[128,4,1024]{2,0,1:T(8,128)(2,1)} %bitcast.363), calls=%async_computation.3 | async-start | bytes 2097152 | tf_op jit(solution)/shard_map/all_to_all | solution.py:150
  186.3 4.6 %convolution_bitcast_fusion.1 = f32[1,1024,1024]{2,1,0:T(8,128)} fusion(bf16[512,1024]{1,0:T(8,128)(2,1)S(1)} %bitcast.369, bf16[512,1024]{1,0:T(8,128)(2,1)} %all-gather.3.cloned.1.call-done), kind=kOutput, calls=%fused_computation.46 | convolution fusion | flops 1073741824 | bytes 6291456 | tf_op jit(solution)/shard_map/dot_general | solution.py:97
  190.9 38.5 %all-to-all-done.3 = bf16[128,4,1024]{2,0,1:T(8,128)(2,1)S(1)} async-done(((bf16[128,4,1024]{2,0,1:T(8,128)(2,1)}), bf16[128,4,1024]{2,0,1:T(8,128)(2,1)S(1)}, u32[]{:S(2)}, u32[]{:S(2)}) %all-to-all-start.3) | async-done | bytes 1048608 | tf_op jit(solution)/shard_map/all_to_all | solution.py:150
  229.4 4.5 %convolution_bitcast_fusion = f32[1,1024,1024]{2,1,0:T(8,128)} fusion(bf16[512,1024]{1,0:T(8,128)(2,1)S(1)} %bitcast.370, bf16[512,1024]{1,0:T(8,128)(2,1)} %all-gather.5.cloned.1.call-done), kind=kOutput, calls=%fused_computation.45 | convolution fusion | flops 1073741824 | bytes 6291456 | tf_op jit(solution)/shard_map/dot_general | solution.py:97
  233.9 2.1 fusion.32
  236.1 1.6 fusion.52
  (75 shorter events, 9.8 us)
Async XLA Ops:
  11.2 5.2 %copy-start.2 = (bf16[1,128,4096]{2,1,0:T(8,128)(2,1)S(1)}, bf16[1,128,4096]{2,1,0:T(8,128)(2,1)}, u32[]{:S(2)}) copy-start(bf16[1,128,4096]{2,1,0:T(8,128)(2,1)} %param.12) | copy-start | bytes 3145732
  11.2 5.2 %copy-start.16 = (bf16[128,4096]{1,0:T(8,128)(2,1)S(1)}, bf16[128,4096]{1,0:T(8,128)(2,1)}, u32[]{:S(2)}) copy-start(bf16[128,4096]{1,0:T(8,128)(2,1)} %param.16) | copy-start | bytes 3145732
  11.2 5.2 %copy-start.17 = (f32[1,4096]{1,0:T(1,128)S(1)}, f32[1,4096]{1,0:T(1,128)}, u32[]{:S(2)}) copy-start(f32[1,4096]{1,0:T(1,128)} %param.13) | copy-start | bytes 49156
  16.4 0.7 copy-start.1
  16.4 1.8 copy-start
  17.1 8.8 %copy-start.3 = (bf16[128,4096]{1,0:T(8,128)(2,1)}, bf16[128,4096]{1,0:T(8,128)(2,1)S(1)}, u32[]{:S(2)}) copy-start(bf16[128,4096]{1,0:T(8,128)(2,1)S(1)} %fusion.53) | copy-start | bytes 3145732
  61.5 2.8 %collective-permute-start = (bf16[16,16,2048]{2,1,0:T(8,128)(2,1)S(1)}, bf16[16,16,2048]{2,1,0:T(8,128)(2,1)}, u32[]{:S(2)}, u32[]{:S(2)}) collective-permute-start(bf16[16,16,2048]{2,1,0:T(8,128)(2,1)S(1)} %all_to_all.45), channel_id=1, source_target_pairs={{0,16},{16,0},{1,17},{17,1},{2,18},{18,2},{3,19},{19,3},{4,20},{20... | collective-permute-start | bytes 3145736 | tf_op jit(solution)/shard_map/ppermute | solution.py:15
  65.5 35.0 %collective-permute-start.1 = (bf16[16,16,2048]{2,1,0:T(8,128)(2,1)S(1)}, bf16[16,16,2048]{2,1,0:T(8,128)(2,1)}, u32[]{:S(2)}, u32[]{:S(2)}) collective-permute-start(bf16[16,16,2048]{2,1,0:T(8,128)(2,1)S(1)} %get-tuple-element.31), channel_id=1, source_target_pairs={{0,16},{16,0},{1,17},{17,1},{2,18},{18,2},{3,19},{19,3},{4,20},{20... | collective-permute-start | bytes 3145736 | tf_op jit(solution)/shard_map/ppermute | solution.py:15
  100.5 30.0 %all-to-all-start.1 = ((bf16[16,16,2048]{2,1,0:T(8,128)(2,1)}), bf16[16,16,2048]{2,1,0:T(8,128)(2,1)S(1)}, u32[]{:S(2)}, u32[]{:S(2)}) async-start(bf16[16,16,2048]{2,1,0:T(8,128)(2,1)} %collective-permute-done.1), calls=%async_computation.1 | async-start | bytes 2097152 | tf_op jit(solution)/shard_map/all_to_all | solution.py:31
  104.0 82.3 %all-gather.3.cloned.1.call-start = ((), (), s32[]{:S(2)}) async-start(), calls=%async_computation.5 | async-start | bytes 1310720 | tf_op jit(solution)/shard_map/all_gather | solution.py:152
  131.6 1.0 copy-start.6
  132.6 96.8 %all-gather.5.cloned.1.call-start = ((), (), s32[]{:S(2)}) async-start(), calls=%async_computation.6 | async-start | bytes 1310720 | tf_op jit(solution)/shard_map/all_gather | solution.py:153
  137.7 3.7 %copy-start.7 = (bf16[128,2048]{1,0:T(8,128)(2,1)S(1)}, bf16[128,2048]{1,0:T(8,128)(2,1)}, u32[]{:S(2)}) copy-start(bf16[128,2048]{1,0:T(8,128)(2,1)} %copy-done.6) | copy-start | bytes 1572868
  137.7 45.0 %all-to-all-start.2 = ((bf16[128,4,1024]{2,0,1:T(8,128)(2,1)}), bf16[128,4,1024]{2,0,1:T(8,128)(2,1)S(1)}, u32[]{:S(2)}, u32[]{:S(2)}) async-start(bf16[128,4,1024]{2,0,1:T(8,128)(2,1)} %fusion.34), calls=%async_computation.2 | async-start | bytes 2097152 | tf_op jit(solution)/shard_map/all_to_all | solution.py:149
  141.4 92.5 %all-reduce.2.cloned.1.call-start = ((), (), s32[]{:S(2)}) async-start(), calls=%async_computation.4 | async-start | bytes 4194304 | tf_op jit(solution)/shard_map/psum | solution.py:146
  155.3 1.2 copy-start.4
  182.7 46.6 %all-to-all-start.3 = ((bf16[128,4,1024]{2,0,1:T(8,128)(2,1)}), bf16[128,4,1024]{2,0,1:T(8,128)(2,1)S(1)}, u32[]{:S(2)}, u32[]{:S(2)}) async-start(bf16[128,4,1024]{2,0,1:T(8,128)(2,1)} %bitcast.363), calls=%async_computation.3 | async-start | bytes 2097152 | tf_op jit(solution)/shard_map/all_to_all | solution.py:150
  233.9 2.2 copy-start.5
Sparse Core Ops, SparseCore 0:
  132.7 46.3 all-gather.2
  180.7 46.8 all-gather.4
Sparse Core Ops, SparseCore 1:
  155.4 70.6 all-reduce.1
where the time goes:
time: 247 us; the launch traced here: 245 us
  waiting for transfers between devices  71.7 us (29%)
  starting transfers between devices  43.4 us (18%)
  other arithmetic  33.2 us (13%)
  matrix products  32.8 us (13%)
  blocking collectives  31.9 us (13%)
  local copies, waits for them, and re-layouts  16.5 us (7%)
  between operations  15.8 us (6%)
    all_to_all x1, waiting for transfers between devices, per_device(): lax.all_to_all(second_left, 'dp', split_axis=1, concat_axis=0, tiled=True)  38.5 us
    ppermute x2, starting transfers between devices, swapped(): lax.ppermute(shard, axis, [(i, i ^ 1 << apart) for i in range(lax.axis_si...  32.6 us
    all_to_all x1, blocking collectives, route(): return lax.all_to_all(slots, 'dp', split_axis=0, concat_axis=0, tiled=True)  31.9 us
    all_to_all x1, waiting for transfers between devices, per_device(): lax.all_to_all(normed, 'dp', split_axis=1, concat_axis=0, tiled=True)  25.1 us
    select_n x1, other arithmetic, unpack(): return padded.reshape(-1, padded.shape[-1])[flat]  20 us
    dot_general x2, matrix products, right_product(): lax.dot_general(rows, weight, (((1,), (1,)), ((), ())), preferred_element...  13.9 us
    dot_general x2, matrix products, left_product(): lax.dot_general(left, right, (((0,), (0,)), ((), ())), preferred_element_...  9.1 us
    dot_general x1, matrix products, per_device(): jnp.dot(normed, weight_a, preferred_element_type=jnp.float32)  5.15 us
  transfers between devices with their start and end apart: 8, of which 5 were waited for; matrix products, arithmetic and copies ran while one was open for 22% of the time, Pallas kernels for 0%

commit v1 on v0

v1 whole, which is shorter than its diff:
```python
import functools

import jax
import jax.numpy as jnp
from jax import lax
from jax.experimental import pallas as pl
from jax.experimental.pallas import tpu as pltpu
from jax.sharding import PartitionSpec as P

HEAD_DIM = 64
LANES = 128
EPS = 1e-06
MESH = pl.DeviceIdType.MESH


def rms_forward(states_row, gain):
    xf = states_row.astype(jnp.float32)
    scale = lax.rsqrt(jnp.mean(xf * xf, axis=-1, keepdims=True) + EPS)
    return (xf, scale, (xf * scale * gain).astype(jnp.bfloat16))


def left_product(left, right):
    return lax.dot_general(
        left, right, (((0,), (0,)), ((), ())), preferred_element_type=jnp.float32
    )


def right_product(rows, weight):
    return lax.dot_general(
        rows, weight, (((1,), (1,)), ((), ())), preferred_element_type=jnp.float32
    )


def sequence_of(lengths, names, tokens):
    slot = jnp.arange(lengths.shape[1], dtype=jnp.int32)
    upto = (slot[:, None] <= slot[None, :]).astype(jnp.int32)
    ends = jnp.sum(lengths[:, :, None] * upto[None], axis=1)
    starts = ends - lengths
    place = jnp.arange(tokens, dtype=jnp.int32)
    inside = (place[None, :, None] >= starts[:, None, :]) & (
        place[None, :, None] < ends[:, None, :]
    )
    return jnp.sum(jnp.where(inside, names[:, None, :], 0), axis=-1).reshape(-1)


def exchange_kernel(
    n, m, paired, normed, second, own_all, other_all, mine_a, mine_b,
    line_send, line_recv, sec_send, sec_recv, za_send, za_recv, mp_send, mp_recv,
    loc_sem,
):
    me = lax.axis_index("dp")
    col = lax.axis_index("mp")
    sec = lax.axis_index("section")
    tokens, width = normed.shape
    part = tokens // m
    cols = width // n
    barrier = pltpu.get_barrier_semaphore()
    for j in range(1, n):
        pl.semaphore_signal(
            barrier, inc=1, device_id={"dp": lax.rem(me + j, n)}, device_id_type=MESH
        )
    for j in range(1, m):
        pl.semaphore_signal(
            barrier, inc=1, device_id={"mp": lax.rem(col + j, m)}, device_id_type=MESH
        )
    pl.semaphore_signal(barrier, inc=1, device_id={"section": 1 - sec}, device_id_type=MESH)
    pl.semaphore_wait(barrier, n + m - 1)

    band = pl.ds(pl.multiple_of(col * part, part), part)

    def line_copy(way, s):
        chunk = me - s if way == 0 else me + s
        target = me + 1 if way == 0 else me - 1
        src = paired if s == 0 else own_all.at[chunk]
        return pltpu.make_async_remote_copy(
            src_ref=src, dst_ref=own_all.at[chunk],
            send_sem=line_send.at[way, s], recv_sem=line_recv.at[way, s],
            device_id={"dp": target}, device_id_type=MESH,
        )

    def line_ok(way, s):
        if way == 0:
            return jnp.logical_and(me - s >= 0, me < n - 1)
        return jnp.logical_and(me + s <= n - 1, me > 0)

    def got(way, s):
        return me - 1 - s >= 0 if way == 0 else me + 1 + s <= n - 1

    def sec_copy(chunk, src):
        return pltpu.make_async_remote_copy(
            src_ref=src, dst_ref=other_all.at[chunk],
            send_sem=sec_send.at[chunk], recv_sem=sec_recv.at[chunk],
            device_id={"section": 1 - sec}, device_id_type=MESH,
        )

    def za_copy(which, j):
        src, dst = ((normed, mine_a), (second, mine_b))[which]
        peer = lax.rem(me + j, n)
        return pltpu.make_async_remote_copy(
            src_ref=src.at[band, pl.ds(pl.multiple_of(peer * cols, cols), cols)],
            dst_ref=dst.at[me, band, :],
            send_sem=za_send.at[which, j], recv_sem=za_recv.at[which, j],
            device_id={"dp": peer}, device_id_type=MESH,
        )

    def mp_copy(which, j):
        dst = (mine_a, mine_b)[which]
        return pltpu.make_async_remote_copy(
            src_ref=dst.at[:, band, :], dst_ref=dst.at[:, band, :],
            send_sem=mp_send.at[which, j], recv_sem=mp_recv.at[which, j],
            device_id={"mp": lax.rem(col + j, m)}, device_id_type=MESH,
        )

    def local(which):
        src, dst = ((normed, mine_a), (second, mine_b))[which]
        return pltpu.make_async_copy(
            src.at[band, pl.ds(pl.multiple_of(me * cols, cols), cols)],
            dst.at[me, band, :], loc_sem.at[which],
        )

    def second_too(fn):
        fn(0)
        pl.when(sec == 1)(lambda: fn(1))

    keep = pltpu.make_async_copy(paired, own_all.at[me], loc_sem.at[2])
    for way in (0, 1):
        pl.when(line_ok(way, 0))(lambda way=way: line_copy(way, 0).start())
    for j in range(1, n):
        second_too(lambda which: za_copy(which, j).start())
    second_too(lambda which: local(which).start())
    keep.start()
    sec_copy(me, paired).start()

    def spread(which):
        local(which).wait()
        for j in range(1, n):
            za_copy(which, j).wait_recv()
        for j in range(1, m):
            mp_copy(which, j).start()

    second_too(spread)

    for s in range(n - 1):
        for way in (0, 1):

            @pl.when(got(way, s))
            def _():
                line_copy(way, s).wait_recv()
                chunk = me - 1 - s if way == 0 else me + 1 + s
                if s + 1 < n - 1:
                    pl.when(line_ok(way, s + 1))(lambda: line_copy(way, s + 1).start())
                sec_copy(chunk, own_all.at[chunk]).start()

    keep.wait()

    def finish(which):
        for j in range(1, n):
            za_copy(which, j).wait_send()
        for j in range(1, m):
            mp_copy(which, j).wait()

    second_too(finish)
    for s in range(n - 1):
        for way in (0, 1):
            pl.when(line_ok(way, s))(lambda way=way, s=s: line_copy(way, s).wait_send())
    for c in range(n):
        sec_copy(c, own_all.at[c]).wait()


def exchange(n, m, paired, normed, second):
    tokens, width = normed.shape
    both = jax.ShapeDtypeStruct((n,) + paired.shape, jnp.bfloat16)
    mine = jax.ShapeDtypeStruct((n, tokens, width // n), jnp.bfloat16)
    dma = pltpu.SemaphoreType.DMA
    return pl.pallas_call(
        functools.partial(exchange_kernel, n, m),
        out_shape=(both, both, mine, mine),
        in_specs=[pl.BlockSpec(memory_space=pltpu.VMEM)] * 3,
        out_specs=[pl.BlockSpec(memory_space=pl.ANY)] * 4,
        scratch_shapes=[
            dma((2, n)), dma((2, n)), dma((n,)), dma((n,)),
            dma((2, n)), dma((2, n)), dma((2, m)), dma((2, m)), dma((3,)),
        ],
        compiler_params=pltpu.CompilerParams(collective_id=0, has_side_effects=True),
        name="exchange",
    )(paired, normed, second)


def attend_kernel(step, qid_col, qid_row, kid_col, kid_row, own_a, own_b, other_a, other_b,
                  out_a, out_b, acc_a, acc_b):
    encoder = lax.axis_index("section") == 0
    rows = own_a.shape[0]
    blocks = rows // step
    lane = lax.broadcasted_iota(jnp.int32, (1, LANES), 1) // HEAD_DIM
    zero = jnp.zeros((), jnp.bfloat16)

    @pl.when(encoder)
    def _():
        keys, values = own_a[...], own_b[...]
        if blocks > 1:
            acc_a[...] = jnp.zeros_like(acc_a)
            acc_b[...] = jnp.zeros_like(acc_b)

        def block(b):
            at = pl.ds(0 if blocks == 1 else pl.multiple_of(b * step, step), step)
            query, dout = other_a[at, :], other_b[at, :]
            mask = kid_col[...] == qid_row[:, at]
            dk, dv = None, None
            for h in range(LANES // HEAD_DIM):
                qh = jnp.where(lane == h, query, zero)
                dh = jnp.where(lane == h, dout, zero)
                score = right_product(keys, qh)
                expo = jnp.exp(jnp.where(mask, score, -jnp.inf))
                weight = expo * (1.0 / jnp.sum(expo, axis=0, keepdims=True))
                dweight = right_product(values, dh)
                total = jnp.sum(weight * dweight, axis=0, keepdims=True)
                dscore = (weight * (dweight - total)).astype(jnp.bfloat16)
                pk = jnp.dot(dscore, qh, preferred_element_type=jnp.float32)
                pv = jnp.dot(weight.astype(jnp.bfloat16), dh, preferred_element_type=jnp.float32)
                dk = pk if dk is None else dk + pk
                dv = pv if dv is None else dv + pv
            if blocks == 1:
                out_a[...] = dk.astype(jnp.bfloat16)
                out_b[...] = dv.astype(jnp.bfloat16)
            else:
                acc_a[...] += dk
                acc_b[...] += dv

        if blocks == 1:
            block(0)
        else:
            pl.loop(0, blocks)(block)
        if blocks > 1:
            out_a[...] = acc_a[...].astype(jnp.bfloat16)
            out_b[...] = acc_b[...].astype(jnp.bfloat16)

    @pl.when(jnp.logical_not(encoder))
    def _():
        keys, values = other_a[...], other_b[...]

        def block(b):
            at = pl.ds(0 if blocks == 1 else pl.multiple_of(b * step, step), step)
            query, dout = own_a[at, :], own_b[at, :]
            mask = qid_col[at, :] == kid_row[...]
            dq, att = None, None
            for h in range(LANES // HEAD_DIM):
                kh = jnp.where(lane == h, keys, zero)
                vh = jnp.where(lane == h, values, zero)
                score = right_product(query, kh)
                expo = jnp.exp(jnp.where(mask, score, -jnp.inf))
                weight = expo * (1.0 / jnp.sum(expo, axis=1, keepdims=True))
                dweight = right_product(dout, vh)
                total = jnp.sum(weight * dweight, axis=1, keepdims=True)
                dscore = (weight * (dweight - total)).astype(jnp.bfloat16)
                pq = jnp.dot(dscore, kh, preferred_element_type=jnp.float32)
                pa = jnp.dot(weight.astype(jnp.bfloat16), vh, preferred_element_type=jnp.float32)
                dq = pq if dq is None else dq + pq
                att = pa if att is None else att + pa
            out_a[at, :] = dq.astype(jnp.bfloat16)
            out_b[at, :] = att.astype(jnp.bfloat16)

        if blocks == 1:
            block(0)
        else:
            pl.loop(0, blocks)(block)


def attend(qid, kid, own, other):
    rows, width = own.shape
    cols = width // 2
    steps = cols // LANES
    step = min(rows, max(LANES, (512 * 512) // rows))
    block = functools.partial(pl.BlockSpec, (rows, LANES))
    col = pl.BlockSpec((rows, 1), lambda i: (0, 0))
    row = pl.BlockSpec((1, rows), lambda i: (0, 0))
    out = jax.ShapeDtypeStruct((rows, cols), jnp.bfloat16)
    return pl.pallas_call(
        functools.partial(attend_kernel, step),
        grid=(steps,),
        out_shape=(out, out),
        in_specs=[col, row, col, row,
                  block(lambda i: (0, i)), block(lambda i: (0, i + steps)),
                  block(lambda i: (0, i)), block(lambda i: (0, i + steps))],
        out_specs=[block(lambda i: (0, i)), block(lambda i: (0, i))],
        scratch_shapes=[pltpu.VMEM((rows, LANES), jnp.float32)] * 2,
        compiler_params=pltpu.CompilerParams(vmem_limit_bytes=60 * 1024 * 1024),
        name="attend",
    )(qid[:, None], qid[None, :], kid[:, None], kid[None, :], own, own, other, other)


def reduce_kernel(m, partial, own, x_ref, gain_ref, out, landed, result, send, recv, osend, orecv, loc):
    col = lax.axis_index("mp")
    tokens = partial.shape[0]
    part = tokens // m
    barrier = pltpu.get_barrier_semaphore()
    for j in range(1, m):
        pl.semaphore_signal(
            barrier, inc=1, device_id={"mp": lax.rem(col + j, m)}, device_id_type=MESH
        )
    pl.semaphore_wait(barrier, m - 1)

    def scatter(j):
        peer = lax.rem(col + j, m)
        return pltpu.make_async_remote_copy(
            src_ref=partial.at[pl.ds(pl.multiple_of(peer * part, part), part), :],
            dst_ref=landed.at[j], send_sem=send.at[j], recv_sem=recv.at[j],
            device_id={"mp": peer}, device_id_type=MESH,
        )

    band = pl.ds(pl.multiple_of(col * part, part), part)

    def gather(j):
        return pltpu.make_async_remote_copy(
            src_ref=result, dst_ref=out.at[band, :],
            send_sem=osend.at[j], recv_sem=orecv.at[j],
            device_id={"mp": lax.rem(col + j, m)}, device_id_type=MESH,
        )

    for j in range(1, m):
        scatter(j).start()
    x = x_ref[band, :].astype(jnp.float32)
    scale = lax.rsqrt(jnp.mean(x * x, axis=-1, keepdims=True) + EPS)
    dnorm = own[...]
    for j in range(1, m):
        scatter(j).wait_recv()
        dnorm = dnorm + landed[j].astype(jnp.float32)
    upper = gain_ref[...] * dnorm
    inner = jnp.mean(x * upper, axis=-1, keepdims=True)
    result[...] = (scale * upper - x * scale * scale * scale * inner).astype(jnp.bfloat16)
    for j in range(1, m):
        gather(j).start()
    keep = pltpu.make_async_copy(result, out.at[band, :], loc)
    keep.start()
    keep.wait()
    for j in range(1, m):
        scatter(j).wait_send()
        gather(j).wait()


def reduce_norm(m, partial, own, states, gain):
    tokens, width = states.shape
    part = tokens // m
    dma = pltpu.SemaphoreType.DMA
    return pl.pallas_call(
        functools.partial(reduce_kernel, m),
        out_shape=jax.ShapeDtypeStruct((tokens, width), jnp.bfloat16),
        in_specs=[pl.BlockSpec(memory_space=pltpu.VMEM)] * 4,
        out_specs=pl.BlockSpec(memory_space=pl.ANY),
        scratch_shapes=[
            pltpu.VMEM((m, part, width), jnp.bfloat16),
            pltpu.VMEM((part, width), jnp.bfloat16),
            dma((m,)), dma((m,)), dma((m,)), dma((m,)), dma,
        ],
        compiler_params=pltpu.CompilerParams(collective_id=1, has_side_effects=True),
        name="reduce_norm",
    )(partial, own, states, gain)


def per_device(states, gains, proj_a, proj_b, cotangent, src_len, tgt_len, dest):
    encoder = lax.axis_index("section") == 0
    member = lax.axis_index("dp")
    n = lax.axis_size("dp")
    m = lax.axis_size("mp")
    gain = gains[0]
    weight_a = proj_a[0]
    weight_b = proj_b[0]
    tokens = states.shape[1]
    _, _, normed = rms_forward(states[0], gain)
    second_left = jnp.where(encoder, normed, cotangent)
    first = jnp.dot(normed, weight_a, preferred_element_type=jnp.float32).astype(jnp.bfloat16)
    second = jnp.dot(second_left, weight_b, preferred_element_type=jnp.float32).astype(jnp.bfloat16)
    paired = jnp.concatenate([first, second], axis=1)
    own, other, mine_a, mine_b = exchange(n, m, paired, normed, second_left)
    rows = n * tokens
    seqs = tgt_len.shape[1]
    names = jnp.arange(n * seqs, dtype=jnp.int32).reshape(n, seqs)
    qid = sequence_of(tgt_len, names, tokens)
    kid = sequence_of(src_len, dest, tokens)
    grad_first, grad_second = attend(
        qid, kid, own.reshape(rows, -1), other.reshape(rows, -1)
    )
    mine_a = mine_a.reshape(rows, -1)
    mine_b = jnp.where(encoder, mine_a, mine_b.reshape(rows, -1))
    own_first = lax.dynamic_slice_in_dim(grad_first, member * tokens, tokens, 0)
    own_second = lax.dynamic_slice_in_dim(grad_second, member * tokens, tokens, 0)
    own_second = jnp.where(encoder, own_second, jnp.zeros((), jnp.bfloat16))
    partial = right_product(own_first, weight_a) + right_product(own_second, weight_b)
    part = tokens // m
    mine = lax.dynamic_slice_in_dim(partial, lax.axis_index("mp") * part, part, 0)
    grad_states = reduce_norm(m, partial.astype(jnp.bfloat16), mine, states[0], gains)
    grad_a = left_product(mine_a, grad_first)
    grad_b = left_product(mine_b, grad_second)
    return (grad_states[None], grad_a[None], grad_b[None])


def solution(mesh):
    return jax.shard_map(
        per_device,
        mesh=mesh,
        in_specs=(
            P("section", "dp", None),
            P("section", None),
            P("section", None, "mp"),
            P("section", None, "mp"),
            P("dp", None),
            P(),
            P(),
            P(),
        ),
        out_specs=(P("section", "dp", None), P("section", "dp", "mp"), P("section", "dp", "mp")),
        check_vma=False,
    )
```

time: 247 us -> 143 us (0.58)
  Pallas kernels: 0 us -> 99.7 us
  waiting for transfers between devices: 71.7 us -> 0 us
  starting transfers between devices: 43.4 us -> 0 us
  blocking collectives: 31.9 us -> 0 us
  other arithmetic: 33.2 us -> 7.06 us
  between operations: 15.8 us -> 0.83 us
  local copies, waits for them, and re-layouts: 16.5 us -> 3.58 us
    pallas_call x0 -> x3, Pallas kernels: none -> 99.7 us  [the longest x1 55.5 us: exchange(): pl.pallas_call(functools.partial(exchange_kernel, n, m), out_shape=(both,...]
    all_to_all x3 -> x0, waiting for transfers between devices: 67.3 us -> none  [the longest x1 38.5 us: per_device(): lax.all_to_all(second_left, 'dp', split_axis=1, concat_axis=0, tiled=True)]
    ppermute x2 -> x0, starting transfers between devices: 32.6 us -> none  [swapped(): lax.ppermute(shard, axis, [(i, i ^ 1 << apart) for i in range(lax.axis_si...]
    all_to_all x1 -> x0, blocking collectives: 31.9 us -> none  [route(): return lax.all_to_all(slots, 'dp', split_axis=0, concat_axis=0, tiled=True)]
    select_n x7 -> x1, other arithmetic: 22.2 us -> 0.25 us  [per_device(): mine_b = jnp.where(encoder, mine_a, mine_b.reshape(rows, -1))]
    all_to_all x3 -> x0, starting transfers between devices: 10.7 us -> none  [the longest x1 3.67 us: per_device(): lax.all_to_all(normed, 'dp', split_axis=1, concat_axis=0, tiled=True)]
    gather x11 -> x0, local copies, waits for them, and re-layouts: 8.01 us -> none  [the longest x1 2.33 us: pack(): taken = rows[jnp.minimum(index, rows.shape[0] - 1)]]
    ppermute x2 -> x0, waiting for transfers between devices: 4.33 us -> none  [swapped(): lax.ppermute(shard, axis, [(i, i ^ 1 << apart) for i in range(lax.axis_si...]
  transfers between devices with their start and end apart: 8 -> 0, of which waited for: 5 -> 0; matrix products, arithmetic and copies ran while one was open for 22% -> 0% of each run, Pallas kernels for 0% -> 0%
where the time goes in v1:
time: 143 us; the launch traced here: 142 us
  Pallas kernels  99.7 us (70%)
  matrix products  30.6 us (21%)
  other arithmetic  7.06 us (5%)
  local copies, waits for them, and re-layouts  3.58 us (3%)
    pallas_call x1, Pallas kernels, exchange(): pl.pallas_call(functools.partial(exchange_kernel, n, m), out_shape=(both,...  55.5 us
    pallas_call x1, Pallas kernels, reduce_norm(): pl.pallas_call(functools.partial(reduce_kernel, m), out_shape=jax.ShapeDt...  26.9 us
    pallas_call x1, Pallas kernels, attend(): pl.pallas_call(functools.partial(attend_kernel, step), grid=(steps,), out...  17.3 us
    dot_general x2, matrix products, right_product(): lax.dot_general(rows, weight, (((1,), (1,)), ((), ())), preferred_element...  13.7 us
    dot_general x2, matrix products, left_product(): lax.dot_general(left, right, (((0,), (0,)), ((), ())), preferred_element_...  6.62 us
    dot_general x1, matrix products, per_device(): jnp.dot(normed, weight_a, preferred_element_type=jnp.float32)  5.16 us
    dot_general x1, matrix products, per_device(): jnp.dot(second_left, weight_b, preferred_element_type=jnp.float32)  5.09 us

profile of v1, /device:TPU:0, one launch (start us, length us, event | category | flops | bytes accessed | tf_op | source)
XLA Modules:
  0.0 141.8 jit_solution(16974353847198826142)
XLA Ops:
  0.6 1.5 %fusion.11 = f32[128]{0:T(128)S(1)} fusion(bf16[1,128,4096]{2,1,0:T(8,128)(2,1)} %param.8), kind=kLoop, calls=%fused_computation.13 | loop fusion | flops 1572736 | bytes 1049088 | tf_op jit(solution)/shard_map/reduce_sum | solution.py:18
  2.2 0.8 multiply_reduce_fusion
  3.0 0.7 sub.7
  3.7 0.7 sub.6
  4.4 0.8 select_reduce_fusion
  5.2 0.0 copy-start.9
  5.2 0.0 copy-start.10
  5.2 0.9 copy.13.qid_col
  6.1 0.9 copy.14.kid_col
  6.9 5.2 %fusion.14 = bf16[128,1024]{1,0:T(8,128)(2,1)S(1)} fusion(bf16[1,4096,1024]{2,1,0:T(8,128)(2,1)} %param.10, bf16[1,128,4096]{2,1,0:T(8,128)(2,1)} %param.8, f32[4096]{0:T(1024)} %bitcast.53, f32[128]{0:T(128)S(1)} %add_rsqrt_fusion), kind=kOutput, calls=%fused_computation.17 | convolution fusion | flops 1075970048 | bytes 9716224 | tf_op jit(solution)/shard_map/dot_general | solution.py:370
  12.1 0.0 copy-done.9
  12.1 0.0 copy-done.10
  12.1 0.0 copy-done.1
  12.1 0.0 copy-done.3
  12.1 0.0 copy-done.6
  12.1 1.5 %broadcast_select_fusion = (bf16[128,4096]{1,0:T(8,128)(2,1)S(1)}, bf16[128,4096]{1,0:T(8,128)(2,1)}) fusion(bf16[128,4096]{1,0:T(8,128)(2,1)S(1)} %copy-done.3, pred[]{:T(512)S(6)} %eq.3, f32[4096]{0:T(1024)S(1)} %bitcast.54, f32[128]{0:T(128)S(1)} %add_rsqrt_fusion, bf16[1,128,4096]{2,1,0:T(8,128)(2,1)S(1)} %copy-done.1), kind=kLoop, calls=%fused_computation.23 | loop fusion | flops 2621440 | bytes 4211201 | tf_op jit(solution)/shard_map/jit(_where)/select_n | solution.py:369
  13.6 5.1 %fusion.17 = bf16[128,1024]{1,0:T(8,128)(2,1)S(1)} fusion(bf16[128,4096]{1,0:T(8,128)(2,1)S(1)} %get-tuple-element.17.second, bf16[1,4096,1024]{2,1,0:T(8,128)(2,1)} %param.11), kind=kOutput, calls=%fused_computation.18 | convolution fusion | flops 1073872896 | bytes 9699328 | tf_op jit(solution)/shard_map/dot_general | solution.py:371
  18.7 0.8 pad_maximum_fusion.paired
  19.6 55.5 %exchange.1 = (bf16[4,128,2048]{2,1,0:T(8,128)(2,1)}, bf16[4,128,2048]{2,1,0:T(8,128)(2,1)}, bf16[4,128,1024]{2,1,0:T(8,128)(2,1)}, bf16[4,128,1024]{2,1,0:T(8,128)(2,1)}) custom-call(bf16[128,2048]{1,0:T(8,128)(2,1)} %pad_maximum_fusion.paired, bf16[128,4096]{1,0:T(8,128)(2,1)} %get-tuple-element.18.normed, bf16[128,4096]{1,0:T(8,128)(2,1)} %copy-done), custom_call_target="tpu_custom_call" | custom-call | tf_op jit(solution)/shard_map/exchange/pallas_call | solution.py:175
  75.1 17.3 %attend.1 = (bf16[512,1024]{1,0:T(8,128)(2,1)}, bf16[512,1024]{1,0:T(8,128)(2,1)}) custom-call(s32[512,1]{1,0:T(8,128)} %copy.13.qid_col, s32[1,512]{1,0:T(1,128)} %bitcast.58, s32[512,1]{1,0:T(8,128)} %copy.14.kid_col, s32[1,512]{1,0:T(1,128)} %bitcast.56, bf16[512,2048]{1,0:T(8,128)(2,1)} %bitcast.47, bf16[512,2048]{1,0:T(8,128)(2,1)} %bitcast.48, ...), custom_call_target="tpu_custom_call" | custom-call | tf_op jit(solution)/shard_map/attend/pallas_call | solution.py:277
  92.4 0.0 copy-done.4
  92.4 0.0 copy-done.5
  92.4 0.2 bitcast_select_fusion
  92.7 0.0 copy-start.8
  92.7 6.5 %fusion = f32[128,4096]{1,0:T(8,128)S(1)} fusion(bf16[1,4096,1024]{2,1,0:T(8,128)(2,1)} %param.11, bf16[512,1024]{1,0:T(8,128)(2,1)} %get-tuple-element.12, s32[]{:T(128)S(6)} %select_n.42, pred[]{:T(512)S(6)} %eq.3), kind=kOutput, calls=%fused_computation | convolution fusion | flops 1073872896 | bytes 10747909 | tf_op jit(solution)/shard_map/dot_general | solution.py:29
  99.2 7.2 %fusion.36 = (bf16[128,4096]{1,0:T(8,128)(2,1)}, f32[128,4096]{1,0:T(8,128)S(1)}) fusion(f32[128,4096]{1,0:T(8,128)S(1)} %fusion, bf16[1,4096,1024]{2,1,0:T(8,128)(2,1)} %param.10, bf16[512,1024]{1,0:T(8,128)(2,1)S(1)} %copy-done.8, s32[]{:T(128)S(6)} %select_n.42), kind=kOutput, calls=%fused_computation.48 | convolution fusion | flops 1074790400 | bytes 13893636 | tf_op jit(solution)/shard_map/dot_general | solution.py:29
  106.4 0.8 constant_dynamic-slice_fusion.own
  107.2 26.9 %reduce_norm.1 = bf16[128,4096]{1,0:T(8,128)(2,1)} custom-call(bf16[128,4096]{1,0:T(8,128)(2,1)} %get-tuple-element.19.partial, f32[32,4096]{1,0:T(8,128)} %constant_dynamic-slice_fusion.own, bf16[128,4096]{1,0:T(8,128)(2,1)} %bitcast.46, f32[1,4096]{1,0:T(1,128)} %gain_ref.1), custom_call_target="tpu_custom_call" | custom-call | tf_op jit(solution)/shard_map/reduce_norm/pallas_call | solution.py:344
  134.2 0.0 copy-start.7
  134.2 3.3 %convolution_bitcast_fusion.1 = f32[1,1024,1024]{2,1,0:T(8,128)} fusion(bf16[512,1024]{1,0:T(8,128)(2,1)S(1)} %bitcast.52, bf16[512,1024]{1,0:T(8,128)(2,1)S(1)} %copy-done.8), kind=kOutput, calls=%fused_computation.12 | convolution fusion | flops 1073741824 | bytes 6291456 | tf_op jit(solution)/shard_map/dot_general | solution.py:23
  137.5 3.3 %convolution_bitcast_fusion = f32[1,1024,1024]{2,1,0:T(8,128)} fusion(bf16[512,1024]{1,0:T(8,128)(2,1)S(1)} %bitcast_select_fusion, bf16[512,1024]{1,0:T(8,128)(2,1)S(1)} %copy-done.7), kind=kOutput, calls=%fused_computation.11 | convolution fusion | flops 1073741824 | bytes 6291456 | tf_op jit(solution)/shard_map/dot_general | solution.py:23
  140.8 1.0 copy.16
  (14 shorter events, 0.0 us)
Async XLA Ops:
  5.2 6.9 %copy-start.9 = (s32[4,128]{1,0:T(4,128)}, s32[4,128]{1,0:T(4,128)S(1)}, u32[]{:S(2)}) copy-start(s32[4,128]{1,0:T(4,128)S(1)} %get-tuple-element.21) | copy-start | bytes 6148
  5.2 6.9 %copy-start.10 = (s32[4,128]{1,0:T(4,128)}, s32[4,128]{1,0:T(4,128)S(1)}, u32[]{:S(2)}) copy-start(s32[4,128]{1,0:T(4,128)S(1)} %get-tuple-element.22) | copy-start | bytes 6148
  6.9 5.2 %copy-start.1 = (bf16[1,128,4096]{2,1,0:T(8,128)(2,1)S(1)}, bf16[1,128,4096]{2,1,0:T(8,128)(2,1)}, u32[]{:S(2)}) copy-start(bf16[1,128,4096]{2,1,0:T(8,128)(2,1)} %param.8) | copy-start | bytes 3145732
  6.9 5.2 %copy-start.3 = (bf16[128,4096]{1,0:T(8,128)(2,1)S(1)}, bf16[128,4096]{1,0:T(8,128)(2,1)}, u32[]{:S(2)}) copy-start(bf16[128,4096]{1,0:T(8,128)(2,1)} %param.12) | copy-start | bytes 3145732
  6.9 5.2 %copy-start.6 = (f32[1,4096]{1,0:T(1,128)S(1)}, f32[1,4096]{1,0:T(1,128)}, u32[]{:S(2)}) copy-start(f32[1,4096]{1,0:T(1,128)} %gain_ref.1) | copy-start | bytes 49156
  13.6 5.1 %copy-start = (bf16[128,4096]{1,0:T(8,128)(2,1)}, bf16[128,4096]{1,0:T(8,128)(2,1)S(1)}, u32[]{:S(2)}) copy-start(bf16[128,4096]{1,0:T(8,128)(2,1)S(1)} %get-tuple-element.17.second) | copy-start | bytes 3145732
  75.1 17.3 %copy-start.4 = (bf16[4,128,1024]{2,1,0:T(8,128)(2,1)S(1)}, bf16[4,128,1024]{2,1,0:T(8,128)(2,1)}, u32[]{:S(2)}) copy-start(bf16[4,128,1024]{2,1,0:T(8,128)(2,1)} %get-tuple-element.13) | copy-start | bytes 3145732
  75.1 17.3 %copy-start.5 = (bf16[4,128,1024]{2,1,0:T(8,128)(2,1)S(1)}, bf16[4,128,1024]{2,1,0:T(8,128)(2,1)}, u32[]{:S(2)}) copy-start(bf16[4,128,1024]{2,1,0:T(8,128)(2,1)} %get-tuple-element.14) | copy-start | bytes 3145732
  92.7 6.5 %copy-start.8 = (bf16[512,1024]{1,0:T(8,128)(2,1)S(1)}, bf16[512,1024]{1,0:T(8,128)(2,1)}, u32[]{:S(2)}) copy-start(bf16[512,1024]{1,0:T(8,128)(2,1)} %get-tuple-element.11) | copy-start | bytes 3145732
  134.2 3.3 %copy-start.7 = (bf16[512,1024]{1,0:T(8,128)(2,1)S(1)}, bf16[512,1024]{1,0:T(8,128)(2,1)}, u32[]{:S(2)}) copy-start(bf16[512,1024]{1,0:T(8,128)(2,1)} %get-tuple-element.12) | copy-start | bytes 3145732
  137.5 3.3 %copy-start.2 = (bf16[128,4096]{1,0:T(8,128)(2,1)S(1)}, bf16[128,4096]{1,0:T(8,128)(2,1)}, u32[]{:S(2)}) copy-start(bf16[128,4096]{1,0:T(8,128)(2,1)} %reduce_norm.1) | copy-start | bytes 3145732

commit v2 on v1

v2 whole, which is shorter than its diff:
```python
import functools

import jax
import jax.numpy as jnp
from jax import lax
from jax.experimental import pallas as pl
from jax.experimental.pallas import tpu as pltpu
from jax.sharding import PartitionSpec as P

HEAD_DIM = 64
LANES = 128
EPS = 1e-06
MESH = pl.DeviceIdType.MESH


def rms_forward(states_row, gain):
    xf = states_row.astype(jnp.float32)
    scale = lax.rsqrt(jnp.mean(xf * xf, axis=-1, keepdims=True) + EPS)
    return (xf, scale, (xf * scale * gain).astype(jnp.bfloat16))


def left_product(left, right):
    return lax.dot_general(
        left, right, (((0,), (0,)), ((), ())), preferred_element_type=jnp.float32
    )


def right_product(rows, weight):
    return lax.dot_general(
        rows, weight, (((1,), (1,)), ((), ())), preferred_element_type=jnp.float32
    )


def sequence_of(lengths, names, tokens):
    slot = jnp.arange(lengths.shape[1], dtype=jnp.int32)
    before = slot[:, None] < slot[None, :]
    starts = jnp.sum(jnp.where(before[None], lengths[:, :, None], 0), axis=1)
    place = jnp.arange(tokens, dtype=jnp.int32)[None, :, None]
    inside = (place >= starts[:, None, :]) & (place < (starts + lengths)[:, None, :])
    return jnp.sum(jnp.where(inside, names[:, None, :], 0), axis=-1).reshape(-1)


def attend_piece(encoder, p, group, id_col, id_row, own, other, out_a, out_b, acc_a, acc_b):
    n, tokens, width = own.shape[1:]
    half = width // 2
    rows = n * tokens
    blocks = n // group
    lane = lax.broadcasted_iota(jnp.int32, (1, LANES), 1) // HEAD_DIM
    zero = jnp.zeros((), jnp.bfloat16)
    f32 = jnp.float32

    def cut(ref, which, c, at):
        lo = pl.multiple_of(which * half + c * LANES, LANES)
        return ref[p, at, :, pl.ds(lo, LANES)].reshape(-1, LANES)

    every = pl.ds(0, n)

    @pl.loop(0, half // LANES)
    def _(c):
        out_cols = pl.ds(pl.multiple_of(p * half + c * LANES, LANES), LANES)

        @pl.when(encoder)
        def _():
            keys, values = cut(own, 0, c, every), cut(own, 1, c, every)
            if blocks > 1:
                acc_a[...] = jnp.zeros_like(acc_a)
                acc_b[...] = jnp.zeros_like(acc_b)

            def block(b):
                at = pl.ds(b * group, group)
                query, dout = cut(other, 0, c, at), cut(other, 1, c, at)
                mask = id_col[...].reshape(rows, 1) == id_row[b]
                dk, dv = None, None
                for h in range(LANES // HEAD_DIM):
                    qh = jnp.where(lane == h, query, zero)
                    dh = jnp.where(lane == h, dout, zero)
                    expo = jnp.exp(jnp.where(mask, right_product(keys, qh), -jnp.inf))
                    weight = expo * (1.0 / jnp.sum(expo, axis=0, keepdims=True))
                    dweight = right_product(values, dh)
                    total = jnp.sum(weight * dweight, axis=0, keepdims=True)
                    dscore = (weight * (dweight - total)).astype(jnp.bfloat16)
                    pk = jnp.dot(dscore, qh, preferred_element_type=f32)
                    pv = jnp.dot(weight.astype(jnp.bfloat16), dh, preferred_element_type=f32)
                    dk = pk if dk is None else dk + pk
                    dv = pv if dv is None else dv + pv
                if blocks == 1:
                    out_a[:, :, out_cols] = dk.astype(jnp.bfloat16).reshape(n, tokens, LANES)
                    out_b[:, :, out_cols] = dv.astype(jnp.bfloat16).reshape(n, tokens, LANES)
                else:
                    acc_a[...] += dk
                    acc_b[...] += dv

            if blocks == 1:
                block(0)
            else:
                pl.loop(0, blocks)(block)
                out_a[:, :, out_cols] = acc_a[...].astype(jnp.bfloat16).reshape(n, tokens, LANES)
                out_b[:, :, out_cols] = acc_b[...].astype(jnp.bfloat16).reshape(n, tokens, LANES)

        @pl.when(jnp.logical_not(encoder))
        def _():
            keys, values = cut(other, 0, c, every), cut(other, 1, c, every)

            def block(b):
                at = pl.ds(b * group, group)
                query, dout = cut(own, 0, c, at), cut(own, 1, c, at)
                ids = id_col[at, :, :].reshape(group * tokens, 1)
                mask = None
                dq, att = None, None
                for h in range(LANES // HEAD_DIM):
                    kh = jnp.where(lane == h, keys, zero)
                    vh = jnp.where(lane == h, values, zero)
                    score = right_product(query, kh)
                    if mask is None:
                        span = group * tokens
                        mask = jnp.concatenate(
                            [ids == id_row[i] for i in range(rows // span)], axis=1
                        )
                    expo = jnp.exp(jnp.where(mask, score, -jnp.inf))
                    weight = expo * (1.0 / jnp.sum(expo, axis=1, keepdims=True))
                    dweight = right_product(dout, vh)
                    total = jnp.sum(weight * dweight, axis=1, keepdims=True)
                    dscore = (weight * (dweight - total)).astype(jnp.bfloat16)
                    pq = jnp.dot(dscore, kh, preferred_element_type=f32)
                    pa = jnp.dot(weight.astype(jnp.bfloat16), vh, preferred_element_type=f32)
                    dq = pq if dq is None else dq + pq
                    att = pa if att is None else att + pa
                shape = (group, tokens, LANES)
                out_a[at, :, out_cols] = dq.astype(jnp.bfloat16).reshape(shape)
                out_b[at, :, out_cols] = att.astype(jnp.bfloat16).reshape(shape)

            if blocks == 1:
                block(0)
            else:
                pl.loop(0, blocks)(block)


def forward_kernel(
    n, m, group, normed, second, id_col, id_row, proj_a, proj_b,
    out_a, out_b, mine_a, mine_b,
    wbuf, paired, own, other, acc_a, acc_b, wsem,
    line_send, line_recv, sec_send, sec_recv, za_send, za_recv, mp_send, mp_recv, loc_sem,
):
    me = lax.axis_index("dp")
    col = lax.axis_index("mp")
    sec = lax.axis_index("section")
    tokens, width = normed.shape
    pieces = wbuf.shape[1]
    half = wbuf.shape[3]
    part = tokens // m
    cols = width // n

    def weight_copy(which, p):
        src = (proj_a, proj_b)[which]
        return pltpu.make_async_copy(
            src.at[0, :, pl.ds(p * half, half)], wbuf.at[which, p], wsem.at[which, p]
        )

    for p in range(pieces):
        for which in (0, 1):
            weight_copy(which, p).start()

    barrier = pltpu.get_barrier_semaphore()
    for j in range(1, n):
        pl.semaphore_signal(
            barrier, inc=1, device_id={"dp": lax.rem(me + j, n)}, device_id_type=MESH
        )
    for j in range(1, m):
        pl.semaphore_signal(
            barrier, inc=1, device_id={"mp": lax.rem(col + j, m)}, device_id_type=MESH
        )
    pl.semaphore_signal(barrier, inc=1, device_id={"section": 1 - sec}, device_id_type=MESH)
    pl.semaphore_wait(barrier, n + m - 1)

    band = pl.ds(pl.multiple_of(col * part, part), part)

    def line_copy(way, s, p):
        chunk = me - s if way == 0 else me + s
        target = me + 1 if way == 0 else me - 1
        src = paired.at[p] if s == 0 else own.at[p, chunk]
        return pltpu.make_async_remote_copy(
            src_ref=src, dst_ref=own.at[p, chunk],
            send_sem=line_send.at[way, s, p], recv_sem=line_recv.at[way, s, p],
            device_id={"dp": target}, device_id_type=MESH,
        )

    def line_ok(way, s):
        if way == 0:
            return jnp.logical_and(me - s >= 0, me < n - 1)
        return jnp.logical_and(me + s <= n - 1, me > 0)

    def got(way, s):
        return me - 1 - s >= 0 if way == 0 else me + 1 + s <= n - 1

    def sec_copy(chunk, p, src):
        return pltpu.make_async_remote_copy(
            src_ref=src, dst_ref=other.at[p, chunk],
            send_sem=sec_send.at[chunk, p], recv_sem=sec_recv.at[chunk, p],
            device_id={"section": 1 - sec}, device_id_type=MESH,
        )

    def za_copy(which, j):
        src, dst = ((normed, mine_a), (second, mine_b))[which]
        peer = lax.rem(me + j, n)
        return pltpu.make_async_remote_copy(
            src_ref=src.at[band, pl.ds(pl.multiple_of(peer * cols, cols), cols)],
            dst_ref=dst.at[me, band, :],
            send_sem=za_send.at[which, j], recv_sem=za_recv.at[which, j],
            device_id={"dp": peer}, device_id_type=MESH,
        )

    def mp_copy(which, j):
        dst = (mine_a, mine_b)[which]
        return pltpu.make_async_remote_copy(
            src_ref=dst.at[:, band, :], dst_ref=dst.at[:, band, :],
            send_sem=mp_send.at[which, j], recv_sem=mp_recv.at[which, j],
            device_id={"mp": lax.rem(col + j, m)}, device_id_type=MESH,
        )

    def local(which):
        src, dst = ((normed, mine_a), (second, mine_b))[which]
        return pltpu.make_async_copy(
            src.at[band, pl.ds(pl.multiple_of(me * cols, cols), cols)],
            dst.at[me, band, :], loc_sem.at[which],
        )

    def keep(p):
        return pltpu.make_async_copy(paired.at[p], own.at[p, me], loc_sem.at[2 + p])

    def second_too(fn):
        fn(0)
        pl.when(sec == 1)(lambda: fn(1))

    for j in range(1, n):
        second_too(lambda which: za_copy(which, j).start())
    second_too(lambda which: local(which).start())

    for p in range(pieces):
        for which in (0, 1):
            weight_copy(which, p).wait()
            rows_in = (normed, second)[which]
            paired[p, :, which * half : (which + 1) * half] = jnp.dot(
                rows_in[...], wbuf[which, p], preferred_element_type=jnp.float32
            ).astype(jnp.bfloat16)
        for way in (0, 1):
            pl.when(line_ok(way, 0))(lambda way=way, p=p: line_copy(way, 0, p).start())
        sec_copy(me, p, paired.at[p]).start()
        keep(p).start()

    def spread(which):
        local(which).wait()
        for j in range(1, n):
            za_copy(which, j).wait_recv()
        for j in range(1, m):
            mp_copy(which, j).start()

    second_too(spread)

    for s in range(n - 1):
        for p in range(pieces):
            for way in (0, 1):

                @pl.when(got(way, s))
                def _():
                    line_copy(way, s, p).wait_recv()
                    chunk = me - 1 - s if way == 0 else me + 1 + s
                    if s + 1 < n - 1:
                        pl.when(line_ok(way, s + 1))(
                            lambda: line_copy(way, s + 1, p).start()
                        )
                    sec_copy(chunk, p, own.at[p, chunk]).start()

            if s == n - 2:
                keep(p).wait()
                for c in range(n):
                    sec_copy(c, p, own.at[p, c]).wait_recv()
                attend_piece(
                    sec == 0, p, group, id_col, id_row, own, other, out_a, out_b, acc_a, acc_b
                )

    def finish(which):
        for j in range(1, n):
            za_copy(which, j).wait_send()
        for j in range(1, m):
            mp_copy(which, j).wait()

    second_too(finish)
    for p in range(pieces):
        for s in range(n - 1):
            for way in (0, 1):
                pl.when(line_ok(way, s))(
                    lambda way=way, s=s, p=p: line_copy(way, s, p).wait_send()
                )
        for c in range(n):
            sec_copy(c, p, own.at[p, c]).wait_send()


def forward(n, m, normed, second, id_c, id_r, proj_a, proj_b):
    tokens, width = normed.shape
    inner = proj_a.shape[2]
    half = 2 * LANES
    pieces = inner // half
    rows = n * tokens
    group = max(1, min(n, 512 * 512 // (rows * tokens)))
    blocks = n // group
    grad = jax.ShapeDtypeStruct((n, tokens, inner), jnp.bfloat16)
    mine = jax.ShapeDtypeStruct((n, tokens, width // n), jnp.bfloat16)
    acc = (rows, LANES) if blocks > 1 else (8, LANES)
    dma = pltpu.SemaphoreType.DMA
    vmem = pl.BlockSpec(memory_space=pltpu.VMEM)
    anyw = pl.BlockSpec(memory_space=pl.ANY)
    bf16 = jnp.bfloat16
    return pl.pallas_call(
        functools.partial(forward_kernel, n, m, group),
        out_shape=(grad, grad, mine, mine),
        in_specs=[vmem] * 4 + [anyw] * 2,
        out_specs=[vmem, vmem, anyw, anyw],
        scratch_shapes=[
            pltpu.VMEM((2, pieces, width, half), bf16),
            pltpu.VMEM((pieces, tokens, 2 * half), bf16),
            pltpu.VMEM((pieces, n, tokens, 2 * half), bf16),
            pltpu.VMEM((pieces, n, tokens, 2 * half), bf16),
            pltpu.VMEM(acc, jnp.float32), pltpu.VMEM(acc, jnp.float32),
            dma((2, pieces)),
            dma((2, n, pieces)), dma((2, n, pieces)), dma((n, pieces)), dma((n, pieces)),
            dma((2, n)), dma((2, n)), dma((2, m)), dma((2, m)), dma((2 + pieces,)),
        ],
        compiler_params=pltpu.CompilerParams(
            collective_id=0, has_side_effects=True, vmem_limit_bytes=67000000
        ),
        name="forward",
    )(normed, second, id_c.reshape(n, tokens, 1), id_r.reshape(blocks, 1, rows // blocks),
      proj_a, proj_b)


def reduce_kernel(m, partial, own, x_ref, gain_ref, out, landed, result, send, recv, osend, orecv, loc):
    col = lax.axis_index("mp")
    tokens = partial.shape[0]
    part = tokens // m
    barrier = pltpu.get_barrier_semaphore()
    for j in range(1, m):
        pl.semaphore_signal(
            barrier, inc=1, device_id={"mp": lax.rem(col + j, m)}, device_id_type=MESH
        )
    pl.semaphore_wait(barrier, m - 1)

    def scatter(j):
        peer = lax.rem(col + j, m)
        return pltpu.make_async_remote_copy(
            src_ref=partial.at[pl.ds(pl.multiple_of(peer * part, part), part), :],
            dst_ref=landed.at[j], send_sem=send.at[j], recv_sem=recv.at[j],
            device_id={"mp": peer}, device_id_type=MESH,
        )

    band = pl.ds(pl.multiple_of(col * part, part), part)

    def gather(j):
        return pltpu.make_async_remote_copy(
            src_ref=result, dst_ref=out.at[band, :],
            send_sem=osend.at[j], recv_sem=orecv.at[j],
            device_id={"mp": lax.rem(col + j, m)}, device_id_type=MESH,
        )

    for j in range(1, m):
        scatter(j).start()
    x = x_ref[band, :].astype(jnp.float32)
    scale = lax.rsqrt(jnp.mean(x * x, axis=-1, keepdims=True) + EPS)
    dnorm = own[...]
    for j in range(1, m):
        scatter(j).wait_recv()
        dnorm = dnorm + landed[j].astype(jnp.float32)
    upper = gain_ref[...] * dnorm
    inner = jnp.mean(x * upper, axis=-1, keepdims=True)
    result[...] = (scale * upper - x * scale * scale * scale * inner).astype(jnp.bfloat16)
    for j in range(1, m):
        gather(j).start()
    keep = pltpu.make_async_copy(result, out.at[band, :], loc)
    keep.start()
    keep.wait()
    for j in range(1, m):
        scatter(j).wait_send()
        gather(j).wait()


def reduce_norm(m, partial, own, states, gain):
    tokens, width = states.shape
    part = tokens // m
    dma = pltpu.SemaphoreType.DMA
    return pl.pallas_call(
        functools.partial(reduce_kernel, m),
        out_shape=jax.ShapeDtypeStruct((tokens, width), jnp.bfloat16),
        in_specs=[pl.BlockSpec(memory_space=pltpu.VMEM)] * 4,
        out_specs=pl.BlockSpec(memory_space=pl.ANY),
        scratch_shapes=[
            pltpu.VMEM((m, part, width), jnp.bfloat16),
            pltpu.VMEM((part, width), jnp.bfloat16),
            dma((m,)), dma((m,)), dma((m,)), dma((m,)), dma,
        ],
        compiler_params=pltpu.CompilerParams(collective_id=1, has_side_effects=True),
        name="reduce_norm",
    )(partial, own, states, gain)


def per_device(states, gains, proj_a, proj_b, cotangent, src_len, tgt_len, dest):
    encoder = lax.axis_index("section") == 0
    member = lax.axis_index("dp")
    n = lax.axis_size("dp")
    m = lax.axis_size("mp")
    gain = gains[0]
    weight_a = proj_a[0]
    weight_b = proj_b[0]
    tokens = states.shape[1]
    _, _, normed = rms_forward(states[0], gain)
    second_left = jnp.where(encoder, normed, cotangent)
    rows = n * tokens
    seqs = tgt_len.shape[1]
    names = jnp.arange(n * seqs, dtype=jnp.int32).reshape(n, seqs)
    qid = sequence_of(tgt_len, names, tokens)
    kid = sequence_of(src_len, dest, tokens)
    grad_first, grad_second, mine_a, mine_b = forward(
        n, m, normed, second_left, jnp.where(encoder, kid, qid), jnp.where(encoder, qid, kid),
        proj_a, proj_b,
    )
    grad_first = grad_first.reshape(rows, -1)
    grad_second = grad_second.reshape(rows, -1)
    mine_a = mine_a.reshape(rows, -1)
    mine_b = jnp.where(encoder, mine_a, mine_b.reshape(rows, -1))
    own_first = lax.dynamic_slice_in_dim(grad_first, member * tokens, tokens, 0)
    own_second = lax.dynamic_slice_in_dim(grad_second, member * tokens, tokens, 0)
    own_second = jnp.where(encoder, own_second, jnp.zeros((), jnp.bfloat16))
    partial = right_product(own_first, weight_a) + right_product(own_second, weight_b)
    part = tokens // m
    mine = lax.dynamic_slice_in_dim(partial, lax.axis_index("mp") * part, part, 0)
    grad_states = reduce_norm(m, partial.astype(jnp.bfloat16), mine, states[0], gains)
    grad_a = left_product(mine_a, grad_first)
    grad_b = left_product(mine_b, grad_second)
    return (grad_states[None], grad_a[None], grad_b[None])


def solution(mesh):
    return jax.shard_map(
        per_device,
        mesh=mesh,
        in_specs=(
            P("section", "dp", None),
            P("section", None),
            P("section", None, "mp"),
            P("section", None, "mp"),
            P("dp", None),
            P(),
            P(),
            P(),
        ),
        out_specs=(P("section", "dp", None), P("section", "dp", "mp"), P("section", "dp", "mp")),
        check_vma=False,
    )
```

time: 143 us -> 126 us (0.88)
  matrix products: 30.6 us -> 21.6 us
  Pallas kernels: 99.7 us -> 92.3 us
    pallas_call x2 -> x1, Pallas kernels: 72.8 us -> 60.6 us  [forward(): pl.pallas_call(functools.partial(forward_kernel, n, m, group), out_shape=...]
    dot_general x2 -> x0, matrix products: 10.2 us -> none  [the longest x1 5.16 us: per_device(): jnp.dot(normed, weight_a, preferred_element_type=jnp.float32)]
    pallas_call x1, Pallas kernels: 26.9 us -> 31.8 us  [reduce_norm(): pl.pallas_call(functools.partial(reduce_kernel, m), out_shape=jax.ShapeDt...]
    another operation x2 -> x0, local copies, waits for them, and re-layouts: 1.73 us -> none  [the longest x1 0.87 us: attend(): qid[:, None]]
where the time goes in v2:
time: 126 us; the launch traced here: 125 us
  Pallas kernels  92.3 us (73%)
  matrix products  21.6 us (17%)
  other arithmetic  7.79 us (6%)
  local copies, waits for them, and re-layouts  2.68 us (2%)
    pallas_call x1, Pallas kernels, forward(): pl.pallas_call(functools.partial(forward_kernel, n, m, group), out_shape=...  60.6 us
    pallas_call x1, Pallas kernels, reduce_norm(): pl.pallas_call(functools.partial(reduce_kernel, m), out_shape=jax.ShapeDt...  31.8 us
    dot_general x2, matrix products, right_product(): lax.dot_general(rows, weight, (((1,), (1,)), ((), ())), preferred_element...  13.7 us
    dot_general x2, matrix products, left_product(): lax.dot_general(left, right, (((0,), (0,)), ((), ())), preferred_element_...  7.86 us
    select_n x1, other arithmetic, per_device(): second_left = jnp.where(encoder, normed, cotangent)  2.6 us

profile of v2, /device:TPU:0, one launch (start us, length us, event | category | flops | bytes accessed | tf_op | source)
XLA Modules:
  0.0 125.1 jit_solution(3798115563138146240)
XLA Ops:
  0.6 0.0 copy-start
  0.7 1.6 %fusion.7 = f32[128]{0:T(128)S(1)} fusion(bf16[1,128,4096]{2,1,0:T(8,128)(2,1)} %param.8), kind=kLoop, calls=%fused_computation.9 | loop fusion | flops 1572736 | bytes 1049088 | tf_op jit(solution)/shard_map/reduce_sum | solution.py:18
  2.3 0.8 select_reduce_fusion.1
  3.1 0.7 add.39
  3.8 0.7 add.38
  4.5 0.8 select_reduce_fusion
  5.3 0.6 broadcast_select_fusion.1
  5.9 0.9 copy.16.id_col
  6.7 0.0 copy-done
  6.7 2.6 %broadcast_select_fusion = (bf16[128,4096]{1,0:T(8,128)(2,1)}, bf16[128,4096]{1,0:T(8,128)(2,1)}) fusion(bf16[128,4096]{1,0:T(8,128)(2,1)} %param.12, pred[]{:T(512)S(6)} %eq.3, f32[4096]{0:T(1024)} %bitcast.34, f32[128]{0:T(128)S(1)} %add_rsqrt_fusion, bf16[1,128,4096]{2,1,0:T(8,128)(2,1)S(1)} %copy-done), kind=kLoop, calls=%fused_computation.14 | loop fusion | flops 2621440 | bytes 4211201 | tf_op jit(solution)/shard_map/jit(_where)/select_n | solution.py:414
  9.3 60.6 %forward.1 = (bf16[4,128,1024]{2,1,0:T(8,128)(2,1)}, bf16[4,128,1024]{2,1,0:T(8,128)(2,1)}, bf16[4,128,1024]{2,1,0:T(8,128)(2,1)}, bf16[4,128,1024]{2,1,0:T(8,128)(2,1)}) custom-call(bf16[128,4096]{1,0:T(8,128)(2,1)} %get-tuple-element.14.normed, bf16[128,4096]{1,0:T(8,128)(2,1)} %get-tuple-element.13.second, s32[4,128,1]{2,1,0:T(8,128)} %copy.16.id_col, ...), custom_call_target="tpu_custom_call" | custom-call | tf_op jit(solution)/shard_map/forward/pallas_call | solution.py:313
  69.9 0.0 copy-start.4
  69.9 6.5 %fusion = f32[128,4096]{1,0:T(8,128)S(1)} fusion(bf16[1,4096,1024]{2,1,0:T(8,128)(2,1)} %proj_b.1, bf16[512,1024]{1,0:T(8,128)(2,1)} %bitcast.33, s32[]{:T(128)S(6)} %select_n.89, pred[]{:T(512)S(6)} %eq.3), kind=kOutput, calls=%fused_computation | convolution fusion | flops 1073872896 | bytes 10747909 | tf_op jit(solution)/shard_map/dot_general | solution.py:29
  76.4 0.0 copy-done.4
  76.4 7.2 %fusion.23 = (bf16[128,4096]{1,0:T(8,128)(2,1)}, f32[128,4096]{1,0:T(8,128)S(1)}) fusion(f32[128,4096]{1,0:T(8,128)S(1)} %fusion, bf16[1,4096,1024]{2,1,0:T(8,128)(2,1)} %proj_a.1, bf16[512,1024]{1,0:T(8,128)(2,1)S(1)} %bitcast.32, s32[]{:T(128)S(6)} %select_n.89), kind=kOutput, calls=%fused_computation.39 | convolution fusion | flops 1074790400 | bytes 13893636 | tf_op jit(solution)/shard_map/dot_general | solution.py:29
  83.7 0.8 constant_dynamic-slice_fusion.own
  84.5 0.0 copy-start.1
  84.5 0.0 copy-start.3
  84.5 31.8 %reduce_norm.1 = bf16[128,4096]{1,0:T(8,128)(2,1)} custom-call(bf16[128,4096]{1,0:T(8,128)(2,1)} %get-tuple-element.17.partial, f32[32,4096]{1,0:T(8,128)} %constant_dynamic-slice_fusion.own, bf16[128,4096]{1,0:T(8,128)(2,1)} %bitcast.30, f32[1,4096]{1,0:T(1,128)} %gain_ref.1), custom_call_target="tpu_custom_call" | custom-call | tf_op jit(solution)/shard_map/reduce_norm/pallas_call | solution.py:389
  116.2 0.0 copy-done.1
  116.3 0.0 copy-done.3
  116.3 4.6 %convolution_bitcast_fusion = f32[1,1024,1024]{2,1,0:T(8,128)} fusion(bf16[4,128,1024]{2,1,0:T(8,128)(2,1)} %get-tuple-element.8, bf16[4,128,1024]{2,1,0:T(8,128)(2,1)S(1)} %copy-done.1, bf16[4,128,1024]{2,1,0:T(8,128)(2,1)S(1)} %copy-done.3, pred[]{:T(512)S(6)} %eq.3), kind=kOutput, calls=%fused_computation.7 | convolution fusion | flops 1074266112 | bytes 7340033 | tf_op jit(solution)/shard_map/dot_general | solution.py:23
  120.8 0.0 copy-start.2
  120.8 3.3 %convolution_bitcast_fusion.1 = f32[1,1024,1024]{2,1,0:T(8,128)} fusion(bf16[4,128,1024]{2,1,0:T(8,128)(2,1)S(1)} %copy-done.1, bf16[4,128,1024]{2,1,0:T(8,128)(2,1)S(1)} %copy-done.4), kind=kOutput, calls=%fused_computation.8 | convolution fusion | flops 1073741824 | bytes 6291456 | tf_op jit(solution)/shard_map/dot_general | solution.py:23
  124.1 0.0 copy-done.2
  124.1 1.0 copy.22
  (3 shorter events, 0.0 us)
Async XLA Ops:
  0.6 6.1 %copy-start = (bf16[1,128,4096]{2,1,0:T(8,128)(2,1)S(1)}, bf16[1,128,4096]{2,1,0:T(8,128)(2,1)}, u32[]{:S(2)}) copy-start(bf16[1,128,4096]{2,1,0:T(8,128)(2,1)} %param.8) | copy-start | bytes 3145732
  69.9 6.5 %copy-start.4 = (bf16[4,128,1024]{2,1,0:T(8,128)(2,1)S(1)}, bf16[4,128,1024]{2,1,0:T(8,128)(2,1)}, u32[]{:S(2)}) copy-start(bf16[4,128,1024]{2,1,0:T(8,128)(2,1)} %get-tuple-element.7) | copy-start | bytes 3145732
  84.5 31.8 %copy-start.1 = (bf16[4,128,1024]{2,1,0:T(8,128)(2,1)S(1)}, bf16[4,128,1024]{2,1,0:T(8,128)(2,1)}, u32[]{:S(2)}) copy-start(bf16[4,128,1024]{2,1,0:T(8,128)(2,1)} %get-tuple-element.9) | copy-start | bytes 3145732
  84.5 31.8 %copy-start.3 = (bf16[4,128,1024]{2,1,0:T(8,128)(2,1)S(1)}, bf16[4,128,1024]{2,1,0:T(8,128)(2,1)}, u32[]{:S(2)}) copy-start(bf16[4,128,1024]{2,1,0:T(8,128)(2,1)} %get-tuple-element.10) | copy-start | bytes 3145732
  120.8 3.3 %copy-start.2 = (bf16[128,4096]{1,0:T(8,128)(2,1)S(1)}, bf16[128,4096]{1,0:T(8,128)(2,1)}, u32[]{:S(2)}) copy-start(bf16[128,4096]{1,0:T(8,128)(2,1)} %reduce_norm.1) | copy-start | bytes 3145732

commit v3 on v2

--- a/solution.py
+++ b/solution.py
@@ -256,8 +256,9 @@
 
     second_too(spread)
 
-    for s in range(n - 1):
-        for p in range(pieces):
+    for wave in range(pieces + n - 2):
+        for s in range(max(0, wave - pieces + 1), min(n - 1, wave + 1)):
+            p = wave - s
             for way in (0, 1):
 
                 @pl.when(got(way, s))
@@ -270,13 +271,14 @@
                         )
                     sec_copy(chunk, p, own.at[p, chunk]).start()
 
-            if s == n - 2:
-                keep(p).wait()
-                for c in range(n):
-                    sec_copy(c, p, own.at[p, c]).wait_recv()
-                attend_piece(
-                    sec == 0, p, group, id_col, id_row, own, other, out_a, out_b, acc_a, acc_b
-                )
+        p = wave - (n - 2)
+        if p >= 0:
+            keep(p).wait()
+            for c in range(n):
+                sec_copy(c, p, own.at[p, c]).wait_recv()
+            attend_piece(
+                sec == 0, p, group, id_col, id_row, own, other, out_a, out_b, acc_a, acc_b
+            )
 
     def finish(which):
         for j in range(1, n):
@@ -308,7 +310,7 @@
     acc = (rows, LANES) if blocks > 1 else (8, LANES)
     dma = pltpu.SemaphoreType.DMA
     vmem = pl.BlockSpec(memory_space=pltpu.VMEM)
-    anyw = pl.BlockSpec(memory_space=pl.ANY)
+    anyw = pl.BlockSpec(memory_space=pltpu.HBM)
     bf16 = jnp.bfloat16
     return pl.pallas_call(
         functools.partial(forward_kernel, n, m, group),
@@ -333,10 +335,34 @@
       proj_a, proj_b)
 
 
-def reduce_kernel(m, partial, own, x_ref, gain_ref, out, landed, result, send, recv, osend, orecv, loc):
+def reduce_kernel(
+    m, grad_a, grad_b, proj_a, proj_b, x_ref, gain_ref, result,
+    left, wbuf, total, mine, partial, landed, gsem, wsem, send, recv,
+):
+    me = lax.axis_index("dp")
     col = lax.axis_index("mp")
-    tokens = partial.shape[0]
+    encoder = lax.axis_index("section") == 0
+    tokens = x_ref.shape[0]
     part = tokens // m
+    chunks, step = wbuf.shape[1:3]
+
+    def left_copy(which):
+        return pltpu.make_async_copy(
+            (grad_a, grad_b)[which].at[me], left.at[which], gsem.at[which]
+        )
+
+    def weight_copy(which, c):
+        return pltpu.make_async_copy(
+            (proj_a, proj_b)[which].at[0, pl.ds(c * step, step), :],
+            wbuf.at[which, c], wsem.at[which, c],
+        )
+
+    left_copy(0).start()
+    pl.when(encoder)(lambda: left_copy(1).start())
+    for c in range(chunks):
+        weight_copy(0, c).start()
+        pl.when(encoder)(lambda c=c: weight_copy(1, c).start())
+
     barrier = pltpu.get_barrier_semaphore()
     for j in range(1, m):
         pl.semaphore_signal(
@@ -344,61 +370,76 @@
         )
     pl.semaphore_wait(barrier, m - 1)
 
-    def scatter(j):
+    def scatter(j, c):
         peer = lax.rem(col + j, m)
+        rows = pl.ds(pl.multiple_of(peer * part, part), part)
+        at = pl.ds(c * step, step)
         return pltpu.make_async_remote_copy(
-            src_ref=partial.at[pl.ds(pl.multiple_of(peer * part, part), part), :],
-            dst_ref=landed.at[j], send_sem=send.at[j], recv_sem=recv.at[j],
+            src_ref=partial.at[rows, at], dst_ref=landed.at[j, :, at],
+            send_sem=send.at[j, c], recv_sem=recv.at[j, c],
             device_id={"mp": peer}, device_id_type=MESH,
         )
 
     band = pl.ds(pl.multiple_of(col * part, part), part)
-
-    def gather(j):
-        return pltpu.make_async_remote_copy(
-            src_ref=result, dst_ref=out.at[band, :],
-            send_sem=osend.at[j], recv_sem=orecv.at[j],
-            device_id={"mp": lax.rem(col + j, m)}, device_id_type=MESH,
-        )
-
-    for j in range(1, m):
-        scatter(j).start()
+    left_copy(0).wait()
+    pl.when(encoder)(lambda: left_copy(1).wait())
+    for c in range(chunks):
+        weight_copy(0, c).wait()
+        total[...] = right_product(left[0], wbuf[0, c])
+
+        @pl.when(encoder)
+        def _():
+            weight_copy(1, c).wait()
+            total[...] += right_product(left[1], wbuf[1, c])
+
+        partial[:, c * step : (c + 1) * step] = total[...].astype(jnp.bfloat16)
+        mine[:, c * step : (c + 1) * step] = total[band, :]
+        for j in range(1, m):
+            scatter(j, c).start()
     x = x_ref[band, :].astype(jnp.float32)
     scale = lax.rsqrt(jnp.mean(x * x, axis=-1, keepdims=True) + EPS)
-    dnorm = own[...]
     for j in range(1, m):
-        scatter(j).wait_recv()
+        for c in range(chunks):
+            scatter(j, c).wait_recv()
+    dnorm = mine[...]
+    for j in range(1, m):
         dnorm = dnorm + landed[j].astype(jnp.float32)
     upper = gain_ref[...] * dnorm
     inner = jnp.mean(x * upper, axis=-1, keepdims=True)
     result[...] = (scale * upper - x * scale * scale * scale * inner).astype(jnp.bfloat16)
     for j in range(1, m):
-        gather(j).start()
-    keep = pltpu.make_async_copy(result, out.at[band, :], loc)
-    keep.start()
-    keep.wait()
-    for j in range(1, m):
-        scatter(j).wait_send()
-        gather(j).wait()
-
-
-def reduce_norm(m, partial, own, states, gain):
+        for c in range(chunks):
+            scatter(j, c).wait_send()
+
+
+def reduce_norm(m, grad_a, grad_b, proj_a, proj_b, states, gain):
     tokens, width = states.shape
+    inner = proj_a.shape[2]
     part = tokens // m
+    step = 4 * LANES
+    chunks = width // step
     dma = pltpu.SemaphoreType.DMA
+    bf16, f32 = jnp.bfloat16, jnp.float32
+    vmem = pl.BlockSpec(memory_space=pltpu.VMEM)
     return pl.pallas_call(
         functools.partial(reduce_kernel, m),
-        out_shape=jax.ShapeDtypeStruct((tokens, width), jnp.bfloat16),
-        in_specs=[pl.BlockSpec(memory_space=pltpu.VMEM)] * 4,
-        out_specs=pl.BlockSpec(memory_space=pl.ANY),
+        out_shape=jax.ShapeDtypeStruct((part, width), bf16),
+        in_specs=[pl.BlockSpec(memory_space=pltpu.HBM)] * 4 + [vmem] * 2,
+        out_specs=vmem,
         scratch_shapes=[
-            pltpu.VMEM((m, part, width), jnp.bfloat16),
-            pltpu.VMEM((part, width), jnp.bfloat16),
-            dma((m,)), dma((m,)), dma((m,)), dma((m,)), dma,
+            pltpu.VMEM((2, tokens, inner), bf16),
+            pltpu.VMEM((2, chunks, step, inner), bf16),
+            pltpu.VMEM((tokens, step), f32),
+            pltpu.VMEM((part, width), f32),
+            pltpu.VMEM((tokens, width), bf16),
+            pltpu.VMEM((m, part, width), bf16),
+            dma((2,)), dma((2, chunks)), dma((m, chunks)), dma((m, chunks)),
         ],
-        compiler_params=pltpu.CompilerParams(collective_id=1, has_side_effects=True),
+        compiler_params=pltpu.CompilerParams(
+            collective_id=1, has_side_effects=True, vmem_limit_bytes=66500000
+        ),
         name="reduce_norm",
-    )(partial, own, states, gain)
+    )(grad_a, grad_b, proj_a, proj_b, states, gain)
 
 
 def per_device(states, gains, proj_a, proj_b, cotangent, src_len, tgt_len, dest):
@@ -421,19 +462,22 @@
         n, m, normed, second_left, jnp.where(encoder, kid, qid), jnp.where(encoder, qid, kid),
         proj_a, proj_b,
     )
-    grad_first = grad_first.reshape(rows, -1)
-    grad_second = grad_second.reshape(rows, -1)
+    mine = reduce_norm(m, grad_first, grad_second, proj_a, proj_b, states[0], gains)
+    col = lax.axis_index("mp")
+    landed = [mine] + [
+        lax.ppermute(mine, "mp", [(i, (i + j) % m) for i in range(m)]) for j in range(1, m)
+    ]
     mine_a = mine_a.reshape(rows, -1)
     mine_b = jnp.where(encoder, mine_a, mine_b.reshape(rows, -1))
-    own_first = lax.dynamic_slice_in_dim(grad_first, member * tokens, tokens, 0)
-    own_second = lax.dynamic_slice_in_dim(grad_second, member * tokens, tokens, 0)
-    own_second = jnp.where(encoder, own_second, jnp.zeros((), jnp.bfloat16))
-    partial = right_product(own_first, weight_a) + right_product(own_second, weight_b)
-    part = tokens // m
-    mine = lax.dynamic_slice_in_dim(partial, lax.axis_index("mp") * part, part, 0)
-    grad_states = reduce_norm(m, partial.astype(jnp.bfloat16), mine, states[0], gains)
-    grad_a = left_product(mine_a, grad_first)
-    grad_b = left_product(mine_b, grad_second)
+    grad_a = left_product(mine_a, grad_first.reshape(rows, -1))
+    grad_b = left_product(mine_b, grad_second.reshape(rows, -1))
+    bands = []
+    for b in range(m):
+        band = landed[0]
+        for j in range(1, m):
+            band = jnp.where(col == (b + j) % m, landed[j], band)
+        bands.append(band)
+    grad_states = jnp.concatenate(bands, axis=0)
     return (grad_states[None], grad_a[None], grad_b[None])
 
 

time: 126 us -> 103 us (0.82)
  matrix products: 21.6 us -> 8.33 us
  Pallas kernels: 92.3 us -> 79.3 us
  starting transfers between devices: 0 us -> 4.23 us
  local copies, waits for them, and re-layouts: 2.68 us -> 0.88 us
    dot_general x2 -> x0, matrix products: 13.7 us -> none  [right_product(): lax.dot_general(rows, weight, (((1,), (1,)), ((), ())), preferred_element...]
    pallas_call x1, Pallas kernels: 31.8 us -> 20.5 us  [reduce_norm(): pl.pallas_call(functools.partial(reduce_kernel, m), out_shape=jax.ShapeDt...]
    ppermute x0 -> x3, starting transfers between devices: none -> 4.23 us  [per_device(): lax.ppermute(mine, 'mp', [(i, (i + j) % m) for i in range(m)])]
    pallas_call x1, Pallas kernels: 60.6 us -> 58.8 us  [forward(): pl.pallas_call(functools.partial(forward_kernel, n, m, group), out_shape=...]
  transfers between devices with their start and end apart: 0 -> 3, of which waited for: 0 -> 0; matrix products, arithmetic and copies ran while one was open for 0% -> 8% of each run, Pallas kernels for 0% -> 0%
where the time goes in v3:
time: 103 us; the launch traced here: 102 us
  Pallas kernels  79.3 us (77%)
  other arithmetic  8.96 us (9%)
  matrix products  8.33 us (8%)
  starting transfers between devices  4.23 us (4%)
    pallas_call x1, Pallas kernels, forward(): pl.pallas_call(functools.partial(forward_kernel, n, m, group), out_shape=...  58.8 us
    pallas_call x1, Pallas kernels, reduce_norm(): pl.pallas_call(functools.partial(reduce_kernel, m), out_shape=jax.ShapeDt...  20.5 us
    dot_general x2, matrix products, left_product(): lax.dot_general(left, right, (((0,), (0,)), ((), ())), preferred_element_...  8.33 us
    ppermute x3, starting transfers between devices, per_device(): lax.ppermute(mine, 'mp', [(i, (i + j) % m) for i in range(m)])  4.23 us
    select_n x1, other arithmetic, per_device(): second_left = jnp.where(encoder, normed, cotangent)  2.6 us
  transfers between devices with their start and end apart: 3, of which 0 were waited for; matrix products, arithmetic and copies ran while one was open for 8% of the time, Pallas kernels for 0%

profile of v3, /device:TPU:0, one launch (start us, length us, event | category | flops | bytes accessed | tf_op | source)
XLA Modules:
  0.0 102.4 jit_solution(7873201582144935868)
XLA Ops:
  0.6 0.0 copy-start
  0.7 1.6 %fusion = f32[128]{0:T(128)S(1)} fusion(bf16[1,128,4096]{2,1,0:T(8,128)(2,1)} %param.8), kind=kLoop, calls=%fused_computation.4 | loop fusion | flops 1572736 | bytes 1049088 | tf_op jit(solution)/shard_map/reduce_sum | solution.py:18
  2.3 0.8 select_reduce_fusion.1
  3.1 0.7 add.29
  3.8 0.7 add.28
  4.5 0.8 select_reduce_fusion
  5.3 0.6 broadcast_select_fusion.1
  5.9 0.9 copy.16.id_col
  6.7 0.0 copy-done
  6.7 2.6 %broadcast_select_fusion = (bf16[128,4096]{1,0:T(8,128)(2,1)}, bf16[128,4096]{1,0:T(8,128)(2,1)}) fusion(bf16[128,4096]{1,0:T(8,128)(2,1)} %param.12, pred[]{:T(512)S(6)} %eq.11, f32[4096]{0:T(1024)} %bitcast.20, f32[128]{0:T(128)S(1)} %add_rsqrt_fusion, bf16[1,128,4096]{2,1,0:T(8,128)(2,1)S(1)} %copy-done), kind=kLoop, calls=%fused_computation.10 | loop fusion | flops 2621440 | bytes 4211201 | tf_op jit(solution)/shard_map/jit(_where)/select_n | solution.py:455
  9.3 58.8 %forward.1 = (bf16[4,128,1024]{2,1,0:T(8,128)(2,1)}, bf16[4,128,1024]{2,1,0:T(8,128)(2,1)}, bf16[4,128,1024]{2,1,0:T(8,128)(2,1)}, bf16[4,128,1024]{2,1,0:T(8,128)(2,1)}) custom-call(bf16[128,4096]{1,0:T(8,128)(2,1)} %get-tuple-element.14.normed, bf16[128,4096]{1,0:T(8,128)(2,1)} %get-tuple-element.13.second, s32[4,128,1]{2,1,0:T(8,128)} %copy.16.id_col, ...), custom_call_target="tpu_custom_call" | custom-call | tf_op jit(solution)/shard_map/forward/pallas_call | solution.py:315
  68.1 20.5 %reduce_norm.1 = bf16[32,4096]{1,0:T(8,128)(2,1)} custom-call(bf16[4,128,1024]{2,1,0:T(8,128)(2,1)} %get-tuple-element.7.grad_a, bf16[4,128,1024]{2,1,0:T(8,128)(2,1)} %get-tuple-element.8.grad_b, bf16[1,4096,1024]{2,1,0:T(8,128)(2,1)} %proj_a.3, bf16[1,4096,1024]{2,1,0:T(8,128)(2,1)} %proj_b.3, bf16[128,4096]{1,0:T(8,128)(2,1)} %bitcast.19, f32[1,4096]{1,0:T(1,128)} %gain_ref.1), custom_call_target="tpu_custom_call" | custom-call | tf_op jit(solution)/shard_map/reduce_norm/pallas_call | solution.py:424
  88.6 1.4 %collective-permute-start.2 = (bf16[32,4096]{1,0:T(8,128)(2,1)}, bf16[32,4096]{1,0:T(8,128)(2,1)S(1)}, u32[]{:S(2)}, u32[]{:S(2)}) collective-permute-start(bf16[32,4096]{1,0:T(8,128)(2,1)} %reduce_norm.1), channel_id=1, source_target_pairs={{0,1},{1,2},{2,3},{3,0},{4,5},{5,6},{6,7},{7,4},{8,9},{9,10},{10,1... | collective-permute-start | bytes 786440 | tf_op jit(solution)/shard_map/ppermute | solution.py:468
  90.0 1.4 %collective-permute-start.1 = (bf16[32,4096]{1,0:T(8,128)(2,1)}, bf16[32,4096]{1,0:T(8,128)(2,1)S(1)}, u32[]{:S(2)}, u32[]{:S(2)}) collective-permute-start(bf16[32,4096]{1,0:T(8,128)(2,1)} %reduce_norm.1), channel_id=1, source_target_pairs={{0,2},{1,3},{2,0},{3,1},{4,6},{5,7},{6,4},{7,5},{8,10},{9,11},{10,... | collective-permute-start | bytes 786440 | tf_op jit(solution)/shard_map/ppermute | solution.py:468
  91.4 1.5 %collective-permute-start = (bf16[32,4096]{1,0:T(8,128)(2,1)}, bf16[32,4096]{1,0:T(8,128)(2,1)S(1)}, u32[]{:S(2)}, u32[]{:S(2)}) collective-permute-start(bf16[32,4096]{1,0:T(8,128)(2,1)} %reduce_norm.1), channel_id=1, source_target_pairs={{0,3},{1,0},{2,1},{3,2},{4,7},{5,4},{6,5},{7,6},{8,11},{9,8},{10,9... | collective-permute-start | bytes 786440 | tf_op jit(solution)/shard_map/ppermute | solution.py:468
  92.8 0.0 copy-start.1
  92.8 0.0 copy-start.2
  92.8 5.0 %convolution_bitcast_fusion = f32[1,1024,1024]{2,1,0:T(8,128)} fusion(bf16[4,128,1024]{2,1,0:T(8,128)(2,1)} %get-tuple-element.8.grad_b, bf16[4,128,1024]{2,1,0:T(8,128)(2,1)} %get-tuple-element.9, bf16[4,128,1024]{2,1,0:T(8,128)(2,1)} %get-tuple-element.10, pred[]{:T(512)S(6)} %eq.11), kind=kOutput, calls=%fused_computation.2 | convolution fusion | flops 1074266112 | bytes 7340033 | tf_op jit(solution)/shard_map/dot_general | solution.py:23
  97.9 0.0 copy-done.1
  97.9 0.0 copy-done.2
  97.9 0.0 copy-start.3
  97.9 3.3 %convolution_bitcast_fusion.1 = f32[1,1024,1024]{2,1,0:T(8,128)} fusion(bf16[4,128,1024]{2,1,0:T(8,128)(2,1)S(1)} %copy-done.1, bf16[4,128,1024]{2,1,0:T(8,128)(2,1)S(1)} %copy-done.2), kind=kOutput, calls=%fused_computation.3 | convolution fusion | flops 1073741824 | bytes 6291456 | tf_op jit(solution)/shard_map/dot_general | solution.py:23
  101.2 0.0 collective-permute-done.2
  101.2 0.0 collective-permute-done.1
  101.2 0.0 collective-permute-done
  101.2 0.0 copy-done.3
  101.2 0.1 select_select_fusion.3
  101.3 1.0 %maximum_bitcast_fusion = bf16[1,128,4096]{2,1,0:T(8,128)(2,1)} fusion(bf16[32,4096]{1,0:T(8,128)(2,1)S(1)} %get-tuple-element.16, bf16[32,4096]{1,0:T(8,128)(2,1)S(1)} %get-tuple-element.17, bf16[32,4096]{1,0:T(8,128)(2,1)S(1)} %get-tuple-element.18, bf16[32,4096]{1,0:T(8,128)(2,1)S(1)} %get-tuple-element.15), kind=kLoop, calls=%fused_computation.7 | loop fusion | flops 4194304 | bytes 2097152 | tf_op jit(solution)/shard_map/broadcast_in_dim | solution.py:481
  (3 shorter events, 0.0 us)
Async XLA Ops:
  0.6 6.1 %copy-start = (bf16[1,128,4096]{2,1,0:T(8,128)(2,1)S(1)}, bf16[1,128,4096]{2,1,0:T(8,128)(2,1)}, u32[]{:S(2)}) copy-start(bf16[1,128,4096]{2,1,0:T(8,128)(2,1)} %param.8) | copy-start | bytes 3145732
  88.6 12.6 %collective-permute-start.2 = (bf16[32,4096]{1,0:T(8,128)(2,1)}, bf16[32,4096]{1,0:T(8,128)(2,1)S(1)}, u32[]{:S(2)}, u32[]{:S(2)}) collective-permute-start(bf16[32,4096]{1,0:T(8,128)(2,1)} %reduce_norm.1), channel_id=1, source_target_pairs={{0,1},{1,2},{2,3},{3,0},{4,5},{5,6},{6,7},{7,4},{8,9},{9,10},{10,1... | collective-permute-start | bytes 786440 | tf_op jit(solution)/shard_map/ppermute | solution.py:468
  90.0 11.2 %collective-permute-start.1 = (bf16[32,4096]{1,0:T(8,128)(2,1)}, bf16[32,4096]{1,0:T(8,128)(2,1)S(1)}, u32[]{:S(2)}, u32[]{:S(2)}) collective-permute-start(bf16[32,4096]{1,0:T(8,128)(2,1)} %reduce_norm.1), channel_id=1, source_target_pairs={{0,2},{1,3},{2,0},{3,1},{4,6},{5,7},{6,4},{7,5},{8,10},{9,11},{10,... | collective-permute-start | bytes 786440 | tf_op jit(solution)/shard_map/ppermute | solution.py:468
  91.4 9.8 %collective-permute-start = (bf16[32,4096]{1,0:T(8,128)(2,1)}, bf16[32,4096]{1,0:T(8,128)(2,1)S(1)}, u32[]{:S(2)}, u32[]{:S(2)}) collective-permute-start(bf16[32,4096]{1,0:T(8,128)(2,1)} %reduce_norm.1), channel_id=1, source_target_pairs={{0,3},{1,0},{2,1},{3,2},{4,7},{5,4},{6,5},{7,6},{8,11},{9,8},{10,9... | collective-permute-start | bytes 786440 | tf_op jit(solution)/shard_map/ppermute | solution.py:468
  92.8 5.0 %copy-start.1 = (bf16[4,128,1024]{2,1,0:T(8,128)(2,1)S(1)}, bf16[4,128,1024]{2,1,0:T(8,128)(2,1)}, u32[]{:S(2)}) copy-start(bf16[4,128,1024]{2,1,0:T(8,128)(2,1)} %get-tuple-element.9) | copy-start | bytes 3145732
  92.8 5.0 %copy-start.2 = (bf16[4,128,1024]{2,1,0:T(8,128)(2,1)S(1)}, bf16[4,128,1024]{2,1,0:T(8,128)(2,1)}, u32[]{:S(2)}) copy-start(bf16[4,128,1024]{2,1,0:T(8,128)(2,1)} %get-tuple-element.7.grad_a) | copy-start | bytes 3145732
  97.9 3.3 %copy-start.3 = (bf16[32,4096]{1,0:T(8,128)(2,1)S(1)}, bf16[32,4096]{1,0:T(8,128)(2,1)}, u32[]{:S(2)}) copy-start(bf16[32,4096]{1,0:T(8,128)(2,1)} %reduce_norm.1) | copy-start | bytes 786436

commit v4 on v3

--- a/solution.py
+++ b/solution.py
@@ -36,7 +36,8 @@
     before = slot[:, None] < slot[None, :]
     starts = jnp.sum(jnp.where(before[None], lengths[:, :, None], 0), axis=1)
     place = jnp.arange(tokens, dtype=jnp.int32)[None, :, None]
-    inside = (place >= starts[:, None, :]) & (place < (starts + lengths)[:, None, :])
+    offset = place - starts[:, None, :]
+    inside = (offset >= 0) & (offset < lengths[:, None, :])
     return jnp.sum(jnp.where(inside, names[:, None, :], 0), axis=-1).reshape(-1)
 
 
@@ -456,11 +457,14 @@
     rows = n * tokens
     seqs = tgt_len.shape[1]
     names = jnp.arange(n * seqs, dtype=jnp.int32).reshape(n, seqs)
-    qid = sequence_of(tgt_len, names, tokens)
-    kid = sequence_of(src_len, dest, tokens)
+    id_c = sequence_of(
+        jnp.where(encoder, src_len, tgt_len), jnp.where(encoder, dest, names), tokens
+    )
+    id_r = sequence_of(
+        jnp.where(encoder, tgt_len, src_len), jnp.where(encoder, names, dest), tokens
+    )
     grad_first, grad_second, mine_a, mine_b = forward(
-        n, m, normed, second_left, jnp.where(encoder, kid, qid), jnp.where(encoder, qid, kid),
-        proj_a, proj_b,
+        n, m, normed, second_left, id_c, id_r, proj_a, proj_b
     )
     mine = reduce_norm(m, grad_first, grad_second, proj_a, proj_b, states[0], gains)
     col = lax.axis_index("mp")

time: 103 us -> 101 us (0.981)
  other arithmetic: 8.96 us -> 6.99 us
    add x2 -> x0, other arithmetic: 1.37 us -> none  [sequence_of(): starts + lengths]
where the time goes in v4:
time: 101 us; the launch traced here: 100 us
  Pallas kernels  79.3 us (79%)
  matrix products  8.32 us (8%)
  other arithmetic  6.99 us (7%)
  starting transfers between devices  4.22 us (4%)
    pallas_call x1, Pallas kernels, forward(): pl.pallas_call(functools.partial(forward_kernel, n, m, group), out_shape=...  58.8 us
    pallas_call x1, Pallas kernels, reduce_norm(): pl.pallas_call(functools.partial(reduce_kernel, m), out_shape=jax.ShapeDt...  20.5 us
    dot_general x2, matrix products, left_product(): lax.dot_general(left, right, (((0,), (0,)), ((), ())), preferred_element_...  8.32 us
    ppermute x3, starting transfers between devices, per_device(): lax.ppermute(mine, 'mp', [(i, (i + j) % m) for i in range(m)])  4.22 us
    select_n x1, other arithmetic, per_device(): second_left = jnp.where(encoder, normed, cotangent)  2.6 us
  transfers between devices with their start and end apart: 3, of which 0 were waited for; matrix products, arithmetic and copies ran while one was open for 8% of the time, Pallas kernels for 0%

profile of v4, /device:TPU:0, one launch (start us, length us, event | category | flops | bytes accessed | tf_op | source)
XLA Modules:
  0.0 100.4 jit_solution(17203409865168713758)
XLA Ops:
  0.6 0.0 copy-start
  0.7 1.6 %fusion = f32[128]{0:T(128)S(1)} fusion(bf16[1,128,4096]{2,1,0:T(8,128)(2,1)} %param.8), kind=kLoop, calls=%fused_computation.4 | loop fusion | flops 1572736 | bytes 1049088 | tf_op jit(solution)/shard_map/reduce_sum | solution.py:18
  2.3 0.7 fusion.11
  3.0 0.1 select_reduce_fusion.1
  3.1 0.1 select_reduce_fusion.2
  3.2 0.9 copy.16.id_col
  4.1 0.7 select_reduce_fusion
  4.8 0.0 copy-done
  4.8 2.6 %broadcast_select_fusion = (bf16[128,4096]{1,0:T(8,128)(2,1)}, bf16[128,4096]{1,0:T(8,128)(2,1)}) fusion(bf16[128,4096]{1,0:T(8,128)(2,1)} %param.12, pred[]{:T(512)S(6)} %eq.11, f32[4096]{0:T(1024)} %bitcast.19, f32[128]{0:T(128)S(1)} %add_rsqrt_fusion, bf16[1,128,4096]{2,1,0:T(8,128)(2,1)S(1)} %copy-done), kind=kLoop, calls=%fused_computation.10 | loop fusion | flops 2621440 | bytes 4211201 | tf_op jit(solution)/shard_map/jit(_where)/select_n | solution.py:456
  7.4 58.8 %forward.1 = (bf16[4,128,1024]{2,1,0:T(8,128)(2,1)}, bf16[4,128,1024]{2,1,0:T(8,128)(2,1)}, bf16[4,128,1024]{2,1,0:T(8,128)(2,1)}, bf16[4,128,1024]{2,1,0:T(8,128)(2,1)}) custom-call(bf16[128,4096]{1,0:T(8,128)(2,1)} %get-tuple-element.14.normed, bf16[128,4096]{1,0:T(8,128)(2,1)} %get-tuple-element.13.second, s32[4,128,1]{2,1,0:T(8,128)} %copy.16.id_col, ...), custom_call_target="tpu_custom_call" | custom-call | tf_op jit(solution)/shard_map/forward/pallas_call | solution.py:316
  66.2 20.5 %reduce_norm.1 = bf16[32,4096]{1,0:T(8,128)(2,1)} custom-call(bf16[4,128,1024]{2,1,0:T(8,128)(2,1)} %get-tuple-element.7.grad_a, bf16[4,128,1024]{2,1,0:T(8,128)(2,1)} %get-tuple-element.8.grad_b, bf16[1,4096,1024]{2,1,0:T(8,128)(2,1)} %proj_a.3, bf16[1,4096,1024]{2,1,0:T(8,128)(2,1)} %proj_b.3, bf16[128,4096]{1,0:T(8,128)(2,1)} %bitcast.18, f32[1,4096]{1,0:T(1,128)} %gain_ref.1), custom_call_target="tpu_custom_call" | custom-call | tf_op jit(solution)/shard_map/reduce_norm/pallas_call | solution.py:425
  86.7 1.4 %collective-permute-start.2 = (bf16[32,4096]{1,0:T(8,128)(2,1)}, bf16[32,4096]{1,0:T(8,128)(2,1)S(1)}, u32[]{:S(2)}, u32[]{:S(2)}) collective-permute-start(bf16[32,4096]{1,0:T(8,128)(2,1)} %reduce_norm.1), channel_id=1, source_target_pairs={{0,1},{1,2},{2,3},{3,0},{4,5},{5,6},{6,7},{7,4},{8,9},{9,10},{10,1... | collective-permute-start | bytes 786440 | tf_op jit(solution)/shard_map/ppermute | solution.py:472
  88.0 1.4 %collective-permute-start.1 = (bf16[32,4096]{1,0:T(8,128)(2,1)}, bf16[32,4096]{1,0:T(8,128)(2,1)S(1)}, u32[]{:S(2)}, u32[]{:S(2)}) collective-permute-start(bf16[32,4096]{1,0:T(8,128)(2,1)} %reduce_norm.1), channel_id=1, source_target_pairs={{0,2},{1,3},{2,0},{3,1},{4,6},{5,7},{6,4},{7,5},{8,10},{9,11},{10,... | collective-permute-start | bytes 786440 | tf_op jit(solution)/shard_map/ppermute | solution.py:472
  89.4 1.5 %collective-permute-start = (bf16[32,4096]{1,0:T(8,128)(2,1)}, bf16[32,4096]{1,0:T(8,128)(2,1)S(1)}, u32[]{:S(2)}, u32[]{:S(2)}) collective-permute-start(bf16[32,4096]{1,0:T(8,128)(2,1)} %reduce_norm.1), channel_id=1, source_target_pairs={{0,3},{1,0},{2,1},{3,2},{4,7},{5,4},{6,5},{7,6},{8,11},{9,8},{10,9... | collective-permute-start | bytes 786440 | tf_op jit(solution)/shard_map/ppermute | solution.py:472
  90.9 0.0 copy-start.1
  90.9 0.0 copy-start.2
  90.9 5.0 %convolution_bitcast_fusion = f32[1,1024,1024]{2,1,0:T(8,128)} fusion(bf16[4,128,1024]{2,1,0:T(8,128)(2,1)} %get-tuple-element.8.grad_b, bf16[4,128,1024]{2,1,0:T(8,128)(2,1)} %get-tuple-element.9, bf16[4,128,1024]{2,1,0:T(8,128)(2,1)} %get-tuple-element.10, pred[]{:T(512)S(6)} %eq.11), kind=kOutput, calls=%fused_computation.2 | convolution fusion | flops 1074266112 | bytes 7340033 | tf_op jit(solution)/shard_map/dot_general | solution.py:23
  95.9 0.0 copy-done.1
  95.9 0.0 copy-done.2
  95.9 0.0 copy-start.3
  95.9 3.3 %convolution_bitcast_fusion.1 = f32[1,1024,1024]{2,1,0:T(8,128)} fusion(bf16[4,128,1024]{2,1,0:T(8,128)(2,1)S(1)} %copy-done.1, bf16[4,128,1024]{2,1,0:T(8,128)(2,1)S(1)} %copy-done.2), kind=kOutput, calls=%fused_computation.3 | convolution fusion | flops 1073741824 | bytes 6291456 | tf_op jit(solution)/shard_map/dot_general | solution.py:23
  99.2 0.0 collective-permute-done.2
  99.2 0.0 collective-permute-done.1
  99.2 0.0 collective-permute-done
  99.2 0.0 copy-done.3
  99.2 0.1 select_select_fusion.3
  99.4 1.0 %maximum_bitcast_fusion = bf16[1,128,4096]{2,1,0:T(8,128)(2,1)} fusion(bf16[32,4096]{1,0:T(8,128)(2,1)S(1)} %get-tuple-element.16, bf16[32,4096]{1,0:T(8,128)(2,1)S(1)} %get-tuple-element.17, bf16[32,4096]{1,0:T(8,128)(2,1)S(1)} %get-tuple-element.18, bf16[32,4096]{1,0:T(8,128)(2,1)S(1)} %get-tuple-element.15), kind=kLoop, calls=%fused_computation.7 | loop fusion | flops 4194304 | bytes 2097152 | tf_op jit(solution)/shard_map/broadcast_in_dim | solution.py:485
  (2 shorter events, 0.0 us)
Async XLA Ops:
  0.6 4.1 %copy-start = (bf16[1,128,4096]{2,1,0:T(8,128)(2,1)S(1)}, bf16[1,128,4096]{2,1,0:T(8,128)(2,1)}, u32[]{:S(2)}) copy-start(bf16[1,128,4096]{2,1,0:T(8,128)(2,1)} %param.8) | copy-start | bytes 3145732
  86.7 12.6 %collective-permute-start.2 = (bf16[32,4096]{1,0:T(8,128)(2,1)}, bf16[32,4096]{1,0:T(8,128)(2,1)S(1)}, u32[]{:S(2)}, u32[]{:S(2)}) collective-permute-start(bf16[32,4096]{1,0:T(8,128)(2,1)} %reduce_norm.1), channel_id=1, source_target_pairs={{0,1},{1,2},{2,3},{3,0},{4,5},{5,6},{6,7},{7,4},{8,9},{9,10},{10,1... | collective-permute-start | bytes 786440 | tf_op jit(solution)/shard_map/ppermute | solution.py:472
  88.0 11.2 %collective-permute-start.1 = (bf16[32,4096]{1,0:T(8,128)(2,1)}, bf16[32,4096]{1,0:T(8,128)(2,1)S(1)}, u32[]{:S(2)}, u32[]{:S(2)}) collective-permute-start(bf16[32,4096]{1,0:T(8,128)(2,1)} %reduce_norm.1), channel_id=1, source_target_pairs={{0,2},{1,3},{2,0},{3,1},{4,6},{5,7},{6,4},{7,5},{8,10},{9,11},{10,... | collective-permute-start | bytes 786440 | tf_op jit(solution)/shard_map/ppermute | solution.py:472
  89.4 9.8 %collective-permute-start = (bf16[32,4096]{1,0:T(8,128)(2,1)}, bf16[32,4096]{1,0:T(8,128)(2,1)S(1)}, u32[]{:S(2)}, u32[]{:S(2)}) collective-permute-start(bf16[32,4096]{1,0:T(8,128)(2,1)} %reduce_norm.1), channel_id=1, source_target_pairs={{0,3},{1,0},{2,1},{3,2},{4,7},{5,4},{6,5},{7,6},{8,11},{9,8},{10,9... | collective-permute-start | bytes 786440 | tf_op jit(solution)/shard_map/ppermute | solution.py:472
  90.9 5.0 %copy-start.1 = (bf16[4,128,1024]{2,1,0:T(8,128)(2,1)S(1)}, bf16[4,128,1024]{2,1,0:T(8,128)(2,1)}, u32[]{:S(2)}) copy-start(bf16[4,128,1024]{2,1,0:T(8,128)(2,1)} %get-tuple-element.9) | copy-start | bytes 3145732
  90.9 5.0 %copy-start.2 = (bf16[4,128,1024]{2,1,0:T(8,128)(2,1)S(1)}, bf16[4,128,1024]{2,1,0:T(8,128)(2,1)}, u32[]{:S(2)}) copy-start(bf16[4,128,1024]{2,1,0:T(8,128)(2,1)} %get-tuple-element.7.grad_a) | copy-start | bytes 3145732
  95.9 3.3 %copy-start.3 = (bf16[32,4096]{1,0:T(8,128)(2,1)S(1)}, bf16[32,4096]{1,0:T(8,128)(2,1)}, u32[]{:S(2)}) copy-start(bf16[32,4096]{1,0:T(8,128)(2,1)} %reduce_norm.1) | copy-start | bytes 786436
